TPU v7x, 32 devices: a whole 2x2x4 slice. The times are simulated.
32 devices in a mesh: groups: 2 (over y), band: 4 (over z), wt: 4 (over x, core).
Axes of the slice: x: 2, y: 2, z: 4, core: 2. Of those that a mesh axis runs over, the one named last changes fastest.
Arguments:
- prior_state: float32 [128, 16, 1024], P('groups', 'band', 'wt'), parts along dimension 0, may hold values from -6 to 6
- langevin_noise: float32 [4, 128, 16, 1024], P(None, 'groups', 'band', 'wt'), parts along dimension 1, may hold values from -6 to 6
- station_values: float32 [8192], P(('groups', 'band', 'wt')), parts along dimension 0, may hold values from -6 to 6
- entry_cell: int32 [8192], P(('groups', 'band', 'wt')), parts along dimension 0, may hold values from 0 to 65535
- entry_owner: int32 [8192], P(('groups', 'band', 'wt')), parts along dimension 0, may hold values from 0 to 3, as said below
- entry_slot: int32 [8192], P(('groups', 'band', 'wt')), parts along dimension 0, may hold values from 0 to 255
- entry_weight: float32 [8192], P(('groups', 'band', 'wt')), parts along dimension 0, may hold values from 0.25 to 1
- live_counts: int32 [32], P(('groups', 'band', 'wt')), parts along dimension 0, may hold values from 64 to 256, as said below
- lift_weight: bfloat16 [64, 256], replicated, may hold values from -0.75 to 0.75
- conv_weight: bfloat16 [9, 256, 256], replicated, may hold values from -0.125 to 0.125
- head_weight: bfloat16 [256, 64], replicated, may hold values from -0.375 to 0.375
- first_gain: float32 [256], replicated, may hold values from 0.1 to 1.9
- second_gain: float32 [256], replicated, may hold values from 0.1 to 1.9
Outputs:
- analysis_state: float32 [128, 16, 1024], P('groups', 'band', 'wt'), parts along dimension 0
- innovation: float32 [8192], P(('groups', 'band', 'wt')), parts along dimension 0
There are 2 independent parts, one for each index of `groups`. A program takes and returns all parts, laid end to end along the dimension named above; an argument that names none is the same for every part. Nothing has to cross between parts.
Inputs may be any that keep to these rules, and one draw needn't show every extreme that they name: `entry_owner`: an entry's owner band lies within 2 bands of the entry's own band; every list holds an entry at offset +2 and one at -2, clipped to the existing bands. `live_counts`: some list is full in every draw.
All inputs are finite; a program needn't handle non-finite values.
Results may differ from a plain program's by a relative error of at most 0.0014.
Values may be sent and summed in bfloat16 or wider, within the bound.
A program may use at most 64 MiB of HBM per device.

v0:
```python
import math

import jax
import jax.numpy as jnp
from jax import lax
from jax.sharding import PartitionSpec as P

REACH = 2


noise_levels = (1.0, 0.6, 0.3)
obs_precision = 4.0
step_factor = 0.1


def with_halo(block, sides, width, periodic):
    for axis, dim in sides:
        count = lax.axis_size(axis)
        forward = [(i, i + 1) for i in range(count - 1)]
        if periodic:
            forward.append((count - 1, 0))
        backward = [(target, source) for source, target in forward]
        low = lax.ppermute(
            lax.slice_in_dim(block, block.shape[dim] - width, None, axis=dim), axis, forward
        )
        high = lax.ppermute(lax.slice_in_dim(block, 0, width, axis=dim), axis, backward)
        block = jnp.concatenate([low, block, high], axis=dim)
    return block


def from_behind(block, axis, distance):
    devices = range(lax.axis_size(axis))
    route = [(i - distance, i) for i in devices if i - distance in devices]
    return lax.ppermute(block, axis, route)


def rms_scale(values, gain):
    power = jnp.mean(values * values, axis=0, keepdims=True)
    return values * lax.rsqrt(power + 1e-06) * gain[:, None, None]


def widened(hidden):
    sideways = with_halo(hidden, (("wt", 2),), 1, True)
    return with_halo(sideways, (("band", 1),), 1, False)


def apply_taps(padded, kernel):
    rows = padded.shape[1] - 2
    cols = padded.shape[2] - 2
    total = jnp.zeros((kernel.shape[2], rows, cols), jnp.float32)
    for tap_index in range(9):
        row_shift, col_shift = divmod(tap_index, 3)
        window = padded[:, row_shift : row_shift + rows, col_shift : col_shift + cols]
        total = total + jnp.einsum(
            "co,chw->ohw", kernel[tap_index], window, preferred_element_type=jnp.float32
        )
    return total


def per_device(
    prior_state,
    langevin_noise,
    station_values,
    entry_cell,
    entry_owner,
    entry_slot,
    entry_weight,
    live_counts,
    lift_weight,
    conv_weight,
    head_weight,
    first_gain,
    second_gain,
):
    count = entry_cell.shape[0]
    stations = station_values.shape[0]
    alive = jnp.arange(count, dtype=jnp.int32) < live_counts[0]
    weights = jnp.where(alive, entry_weight, jnp.float32(0.0))
    my_band = lax.axis_index("band")
    offset = entry_owner - my_band + REACH
    near_index = offset * stations + entry_slot

    def evaluate(current, level):
        scaled = (current / math.sqrt(1.0 + level * level)).astype(jnp.bfloat16)
        lifted = jnp.einsum("vo,vhw->ohw", lift_weight, scaled, preferred_element_type=jnp.float32)
        first = jax.nn.silu(rms_scale(lifted, first_gain)).astype(jnp.bfloat16)
        padded = widened(first)
        mixed = lifted + apply_taps(padded, conv_weight)
        second = jax.nn.silu(rms_scale(mixed, second_gain)).astype(jnp.bfloat16)
        score = (
            jnp.einsum("co,chw->ohw", head_weight, second, preferred_element_type=jnp.float32)
            / level
        )
        values = weights * current.reshape(-1)[entry_cell]
        buffer = jnp.zeros(((2 * REACH + 1) * stations,), jnp.float32).at[near_index].add(values)
        buffer = buffer.reshape(2 * REACH + 1, stations)
        interp = buffer[REACH]
        upward = buffer[REACH + 1 :]
        downward = buffer[:REACH][::-1]
        for hop in range(REACH):
            arrived_up = from_behind(upward, "band", 1)
            arrived_down = from_behind(downward, "band", -1)
            interp = interp + arrived_up[0] + arrived_down[0]
            upward = arrived_up[1:]
            downward = arrived_down[1:]
        innov = station_values - interp
        below = []
        above = []
        lower_value = innov
        upper_value = innov
        for hop in range(REACH):
            lower_value = from_behind(lower_value, "band", 1)
            upper_value = from_behind(upper_value, "band", -1)
            below.append(lower_value)
            above.append(upper_value)
        pieces = below[::-1] + [innov] + above
        back = jnp.stack(pieces).reshape(-1)[near_index]
        adjoint = jnp.zeros((current.size,), jnp.float32).at[entry_cell].add(weights * back)
        return (score + obs_precision * adjoint.reshape(current.shape), innov)

    current = prior_state
    innov = station_values
    for section in range(2):
        upper = noise_levels[section]
        lower = noise_levels[section + 1]
        spread = upper * upper - lower * lower
        drift, innov = evaluate(current, upper)
        current = current + spread * drift + math.sqrt(spread) * langevin_noise[2 * section]
        factor = step_factor * lower * lower
        drift, innov = evaluate(current, lower)
        current = (
            current + factor * drift + math.sqrt(2.0 * factor) * langevin_noise[2 * section + 1]
        )
    return (current, innov)


def solution(mesh):
    in_specs = (
        P("groups", "band", "wt"),
        P(None, "groups", "band", "wt"),
        P(("groups", "band", "wt")),
        P(("groups", "band", "wt")),
        P(("groups", "band", "wt")),
        P(("groups", "band", "wt")),
        P(("groups", "band", "wt")),
        P(("groups", "band", "wt")),
        P(),
        P(),
        P(),
        P(),
        P(),
    )
    out_specs = (P("groups", "band", "wt"), P(("groups", "band", "wt")))
    return jax.shard_map(
        per_device, mesh=mesh, in_specs=in_specs, out_specs=out_specs, check_vma=False
    )
```

profile of v0, /device:TPU:0, one launch (start us, length us, event | category | flops | bytes accessed | tf_op | source)
XLA Modules:
  0.0 210.1 jit_solution(5459529131440576998)
XLA Ops:
  3.2 1.7 gather_fusion
  5.0 2.0 scatter_custom_fusion
  8.4 5.6 %collective-permute-start.4 = (f32[2,256]{1,0:T(2,128)S(1)}, f32[2,256]{1,0:T(2,128)S(1)}, u32[]{:S(2)}, u32[]{:S(2)}) collective-permute-start(f32[2,256]{1,0:T(2,128)S(1)} %slice.441), channel_id=1, source_target_pairs={{0,4},{4,8},{8,12},{1,5},{5,9},{9,13},{2,6},{6,10},{10,14},{3,7},{... | collective-permute-start | bytes 6152 | tf_op jit(solution)/shard_map/ppermute | solution.py:34
  15.1 1.7 collective-permute-start.1
  16.8 1.3 fusion.180
  20.5 4.6 %collective-permute-start.6 = (f32[1,256]{1,0:T(1,128)S(1)}, f32[1,256]{1,0:T(1,128)S(1)}, u32[]{:S(2)}, u32[]{:S(2)}) collective-permute-start(f32[1,256]{1,0:T(1,128)S(1)} %get-tuple-element.57), channel_id=1, source_target_pairs={{0,4},{4,8},{8,12},{1,5},{5,9},{9,13},{2,6},{6,10},{10,14},{3,7},{... | collective-permute-start | bytes 3080 | tf_op jit(solution)/shard_map/ppermute | solution.py:34
  27.6 4.8 %collective-permute-start.8 = (f32[256]{0:T(256)S(1)}, f32[256]{0:T(256)S(1)}, u32[]{:S(2)}, u32[]{:S(2)}) collective-permute-start(f32[256]{0:T(256)S(1)} %fusion.278), channel_id=1, source_target_pairs={{0,4},{4,8},{8,12},{1,5},{5,9},{9,13},{2,6},{6,10},{10,14},{3,7},{... | collective-permute-start | bytes 3080 | tf_op jit(solution)/shard_map/ppermute | solution.py:34
  33.2 3.9 %collective-permute-start.2 = (bf16[256,1,258]{0,2,1:T(8,128)(2,1)}, bf16[256,1,258]{0,2,1:T(8,128)(2,1)S(1)}, u32[]{:S(2)}, u32[]{:S(2)}) collective-permute-start(bf16[256,1,258]{0,2,1:T(8,128)(2,1)} %get-tuple-element.26), channel_id=1, source_target_pairs={{0,4},{4,8},{8,12},{1,5},{5,9},{9,13},{2,6},{6,10},{10,14},{3,7},{... | collective-permute-start | bytes 396296 | tf_op jit(solution)/shard_map/ppermute | solution.py:23
  39.8 5.2 %collective-permute-start.9 = (f32[256]{0:T(256)S(1)}, f32[256]{0:T(256)S(1)}, u32[]{:S(2)}, u32[]{:S(2)}) collective-permute-start(f32[256]{0:T(256)S(1)} %collective-permute-done.8), channel_id=1, source_target_pairs={{0,4},{4,8},{8,12},{1,5},{5,9},{9,13},{2,6},{6,10},{10,14},{3,7},{... | collective-permute-start | bytes 3080 | tf_op jit(solution)/shard_map/ppermute | solution.py:34
  45.0 1.3 fusion.132
  46.3 1.7 gather_fusion.1
  48.1 2.0 scatter_custom_fusion.1
  58.2 1.7 gather_fusion.2
  59.9 2.0 scatter_custom_fusion.2
  63.4 4.8 %collective-permute-start.16 = (f32[2,256]{1,0:T(2,128)S(1)}, f32[2,256]{1,0:T(2,128)S(1)}, u32[]{:S(2)}, u32[]{:S(2)}) collective-permute-start(f32[2,256]{1,0:T(2,128)S(1)} %slice.463), channel_id=1, source_target_pairs={{0,4},{4,8},{8,12},{1,5},{5,9},{9,13},{2,6},{6,10},{10,14},{3,7},{... | collective-permute-start | bytes 6152 | tf_op jit(solution)/shard_map/ppermute | solution.py:34
  68.6 1.3 fusion.178
  71.2 4.8 %collective-permute-start.18 = (f32[1,256]{1,0:T(1,128)S(1)}, f32[1,256]{1,0:T(1,128)S(1)}, u32[]{:S(2)}, u32[]{:S(2)}) collective-permute-start(f32[1,256]{1,0:T(1,128)S(1)} %get-tuple-element.53), channel_id=1, source_target_pairs={{0,4},{4,8},{8,12},{1,5},{5,9},{9,13},{2,6},{6,10},{10,14},{3,7},{... | collective-permute-start | bytes 3080 | tf_op jit(solution)/shard_map/ppermute | solution.py:34
  76.1 1.7 collective-permute-start.13
  79.2 4.7 %collective-permute-start.20 = (f32[256]{0:T(256)S(1)}, f32[256]{0:T(256)S(1)}, u32[]{:S(2)}, u32[]{:S(2)}) collective-permute-start(f32[256]{0:T(256)S(1)} %fusion.274), channel_id=1, source_target_pairs={{0,4},{4,8},{8,12},{1,5},{5,9},{9,13},{2,6},{6,10},{10,14},{3,7},{... | collective-permute-start | bytes 3080 | tf_op jit(solution)/shard_map/ppermute | solution.py:34
  84.7 3.9 %collective-permute-start.14 = (bf16[256,1,258]{0,2,1:T(8,128)(2,1)}, bf16[256,1,258]{0,2,1:T(8,128)(2,1)S(1)}, u32[]{:S(2)}, u32[]{:S(2)}) collective-permute-start(bf16[256,1,258]{0,2,1:T(8,128)(2,1)} %get-tuple-element.22), channel_id=1, source_target_pairs={{0,4},{4,8},{8,12},{1,5},{5,9},{9,13},{2,6},{6,10},{10,14},{3,7},{... | collective-permute-start | bytes 396296 | tf_op jit(solution)/shard_map/ppermute | solution.py:23
  91.3 5.2 %collective-permute-start.21 = (f32[256]{0:T(256)S(1)}, f32[256]{0:T(256)S(1)}, u32[]{:S(2)}, u32[]{:S(2)}) collective-permute-start(f32[256]{0:T(256)S(1)} %collective-permute-done.20), channel_id=1, source_target_pairs={{0,4},{4,8},{8,12},{1,5},{5,9},{9,13},{2,6},{6,10},{10,14},{3,7},{... | collective-permute-start | bytes 3080 | tf_op jit(solution)/shard_map/ppermute | solution.py:34
  96.4 1.3 fusion.118
  97.8 1.7 gather_fusion.3
  99.5 2.0 scatter_custom_fusion.3
  108.8 1.7 gather_fusion.4
  110.6 2.0 scatter_custom_fusion.4
  114.1 4.8 %collective-permute-start.28 = (f32[2,256]{1,0:T(2,128)S(1)}, f32[2,256]{1,0:T(2,128)S(1)}, u32[]{:S(2)}, u32[]{:S(2)}) collective-permute-start(f32[2,256]{1,0:T(2,128)S(1)} %slice.485), channel_id=1, source_target_pairs={{0,4},{4,8},{8,12},{1,5},{5,9},{9,13},{2,6},{6,10},{10,14},{3,7},{... | collective-permute-start | bytes 6152 | tf_op jit(solution)/shard_map/ppermute | solution.py:34
  119.2 1.3 fusion.176
  121.9 4.8 %collective-permute-start.30 = (f32[1,256]{1,0:T(1,128)S(1)}, f32[1,256]{1,0:T(1,128)S(1)}, u32[]{:S(2)}, u32[]{:S(2)}) collective-permute-start(f32[1,256]{1,0:T(1,128)S(1)} %get-tuple-element.49), channel_id=1, source_target_pairs={{0,4},{4,8},{8,12},{1,5},{5,9},{9,13},{2,6},{6,10},{10,14},{3,7},{... | collective-permute-start | bytes 3080 | tf_op jit(solution)/shard_map/ppermute | solution.py:34
  126.8 1.7 collective-permute-start.25
  129.8 4.6 %collective-permute-start.32 = (f32[256]{0:T(256)S(1)}, f32[256]{0:T(256)S(1)}, u32[]{:S(2)}, u32[]{:S(2)}) collective-permute-start(f32[256]{0:T(256)S(1)} %fusion.270), channel_id=1, source_target_pairs={{0,4},{4,8},{8,12},{1,5},{5,9},{9,13},{2,6},{6,10},{10,14},{3,7},{... | collective-permute-start | bytes 3080 | tf_op jit(solution)/shard_map/ppermute | solution.py:34
  135.2 3.9 %collective-permute-start.26 = (bf16[256,1,258]{0,2,1:T(8,128)(2,1)}, bf16[256,1,258]{0,2,1:T(8,128)(2,1)S(1)}, u32[]{:S(2)}, u32[]{:S(2)}) collective-permute-start(bf16[256,1,258]{0,2,1:T(8,128)(2,1)} %get-tuple-element.18), channel_id=1, source_target_pairs={{0,4},{4,8},{8,12},{1,5},{5,9},{9,13},{2,6},{6,10},{10,14},{3,7},{... | collective-permute-start | bytes 396296 | tf_op jit(solution)/shard_map/ppermute | solution.py:23
  141.7 5.2 %collective-permute-start.33 = (f32[256]{0:T(256)S(1)}, f32[256]{0:T(256)S(1)}, u32[]{:S(2)}, u32[]{:S(2)}) collective-permute-start(f32[256]{0:T(256)S(1)} %collective-permute-done.32), channel_id=1, source_target_pairs={{0,4},{4,8},{8,12},{1,5},{5,9},{9,13},{2,6},{6,10},{10,14},{3,7},{... | collective-permute-start | bytes 3080 | tf_op jit(solution)/shard_map/ppermute | solution.py:34
  146.9 1.3 fusion.104
  148.2 1.7 gather_fusion.5
  150.0 2.2 %scatter_custom_fusion.5 = f32[65536]{0:T(1024)S(1)} fusion(s32[256]{0:T(256)S(1)} %compare_select_fusion.1, f32[256]{0:T(256)S(1)} %mul.332, f32[]{:T(128)} %constant.26.clone.1), kind=kCustom, calls=%fused_computation.296 | custom fusion | flops 256 | bytes 262148 | tf_op jit(solution)/shard_map/scatter-add | solution.py:118
  159.5 1.7 gather_fusion.6
  161.2 2.0 scatter_custom_fusion.6
  164.7 4.8 %collective-permute-start.40 = (f32[2,256]{1,0:T(2,128)S(1)}, f32[2,256]{1,0:T(2,128)S(1)}, u32[]{:S(2)}, u32[]{:S(2)}) collective-permute-start(f32[2,256]{1,0:T(2,128)S(1)} %slice.507), channel_id=1, source_target_pairs={{0,4},{4,8},{8,12},{1,5},{5,9},{9,13},{2,6},{6,10},{10,14},{3,7},{... | collective-permute-start | bytes 6152 | tf_op jit(solution)/shard_map/ppermute | solution.py:34
  169.9 1.3 fusion.174
  172.5 4.8 %collective-permute-start.42 = (f32[1,256]{1,0:T(1,128)S(1)}, f32[1,256]{1,0:T(1,128)S(1)}, u32[]{:S(2)}, u32[]{:S(2)}) collective-permute-start(f32[1,256]{1,0:T(1,128)S(1)} %get-tuple-element.45), channel_id=1, source_target_pairs={{0,4},{4,8},{8,12},{1,5},{5,9},{9,13},{2,6},{6,10},{10,14},{3,7},{... | collective-permute-start | bytes 3080 | tf_op jit(solution)/shard_map/ppermute | solution.py:34
  177.4 1.7 collective-permute-start.37
  180.5 4.6 %collective-permute-start.44 = (f32[256]{0:T(256)S(1)}, f32[256]{0:T(256)S(1)}, u32[]{:S(2)}, u32[]{:S(2)}) collective-permute-start(f32[256]{0:T(256)S(1)} %fusion.266), channel_id=1, source_target_pairs={{0,4},{4,8},{8,12},{1,5},{5,9},{9,13},{2,6},{6,10},{10,14},{3,7},{... | collective-permute-start | bytes 3080 | tf_op jit(solution)/shard_map/ppermute | solution.py:34
  185.8 3.9 %collective-permute-start.38 = (bf16[256,1,258]{0,2,1:T(8,128)(2,1)}, bf16[256,1,258]{0,2,1:T(8,128)(2,1)S(1)}, u32[]{:S(2)}, u32[]{:S(2)}) collective-permute-start(bf16[256,1,258]{0,2,1:T(8,128)(2,1)} %get-tuple-element.14), channel_id=1, source_target_pairs={{0,4},{4,8},{8,12},{1,5},{5,9},{9,13},{2,6},{6,10},{10,14},{3,7},{... | collective-permute-start | bytes 396296 | tf_op jit(solution)/shard_map/ppermute | solution.py:23
  192.4 5.2 %collective-permute-start.45 = (f32[256]{0:T(256)S(1)}, f32[256]{0:T(256)S(1)}, u32[]{:S(2)}, u32[]{:S(2)}) collective-permute-start(f32[256]{0:T(256)S(1)} %collective-permute-done.44), channel_id=1, source_target_pairs={{0,4},{4,8},{8,12},{1,5},{5,9},{9,13},{2,6},{6,10},{10,14},{3,7},{... | collective-permute-start | bytes 3080 | tf_op jit(solution)/shard_map/ppermute | solution.py:34
  197.6 1.3 fusion.90
  198.9 1.7 gather_fusion.7
  200.7 2.0 scatter_custom_fusion.7
  (264 shorter events, 65.6 us)
Async XLA Ops:
  7.1 12.0 %collective-permute-start.5 = (f32[2,256]{1,0:T(2,128)S(1)}, f32[2,256]{1,0:T(2,128)S(1)}, u32[]{:S(2)}, u32[]{:S(2)}) collective-permute-start(f32[2,256]{1,0:T(2,128)S(1)} %rev.12), channel_id=1, source_target_pairs={{4,0},{8,4},{12,8},{5,1},{9,5},{13,9},{6,2},{10,6},{14,10},{7,3},{... | collective-permute-start | bytes 6152 | tf_op jit(solution)/shard_map/ppermute | solution.py:34
  8.4 12.0 %collective-permute-start.4 = (f32[2,256]{1,0:T(2,128)S(1)}, f32[2,256]{1,0:T(2,128)S(1)}, u32[]{:S(2)}, u32[]{:S(2)}) collective-permute-start(f32[2,256]{1,0:T(2,128)S(1)} %slice.441), channel_id=1, source_target_pairs={{0,4},{4,8},{8,12},{1,5},{5,9},{9,13},{2,6},{6,10},{10,14},{3,7},{... | collective-permute-start | bytes 6152 | tf_op jit(solution)/shard_map/ppermute | solution.py:34
  15.0 17.4 %collective-permute-start = (bf16[256,4,1]{0,2,1:T(2,128)(2,1)S(1)}, bf16[256,4,1]{0,2,1:T(2,128)(2,1)S(1)}, u32[]{:S(2)}, u32[]{:S(2)}) collective-permute-start(bf16[256,4,1]{0,2,1:T(2,128)(2,1)S(1)} %get-tuple-element.34), channel_id=1, source_target_pairs={{0,1},{1,2},{2,3},{3,0},{4,5},{5,6},{6,7},{7,4},{8,9},{9,10},{10,1... | collective-permute-start | bytes 6152 | tf_op jit(solution)/shard_map/ppermute | solution.py:23
  15.1 17.4 %collective-permute-start.1 = (bf16[256,4,1]{0,2,1:T(2,128)(2,1)S(1)}, bf16[256,4,1]{0,2,1:T(2,128)(2,1)S(1)}, u32[]{:S(2)}, u32[]{:S(2)}) collective-permute-start(bf16[256,4,1]{0,2,1:T(2,128)(2,1)S(1)} %get-tuple-element.35), channel_id=1, source_target_pairs={{1,0},{2,1},{3,2},{0,3},{5,4},{6,5},{7,6},{4,7},{9,8},{10,9},{11,1... | collective-permute-start | bytes 6152 | tf_op jit(solution)/shard_map/ppermute | solution.py:26
  19.2 5.9 %collective-permute-start.7 = (f32[1,256]{1,0:T(1,128)S(1)}, f32[1,256]{1,0:T(1,128)S(1)}, u32[]{:S(2)}, u32[]{:S(2)}) collective-permute-start(f32[1,256]{1,0:T(1,128)S(1)} %get-tuple-element.59), channel_id=1, source_target_pairs={{4,0},{8,4},{12,8},{5,1},{9,5},{13,9},{6,2},{10,6},{14,10},{7,3},{... | collective-permute-start | bytes 3080 | tf_op jit(solution)/shard_map/ppermute | solution.py:34
  20.5 5.8 %collective-permute-start.6 = (f32[1,256]{1,0:T(1,128)S(1)}, f32[1,256]{1,0:T(1,128)S(1)}, u32[]{:S(2)}, u32[]{:S(2)}) collective-permute-start(f32[1,256]{1,0:T(1,128)S(1)} %get-tuple-element.57), channel_id=1, source_target_pairs={{0,4},{4,8},{8,12},{1,5},{5,9},{9,13},{2,6},{6,10},{10,14},{3,7},{... | collective-permute-start | bytes 3080 | tf_op jit(solution)/shard_map/ppermute | solution.py:34
  26.3 12.1 %collective-permute-start.10 = (f32[256]{0:T(256)S(1)}, f32[256]{0:T(256)S(1)}, u32[]{:S(2)}, u32[]{:S(2)}) collective-permute-start(f32[256]{0:T(256)S(1)} %fusion.278), channel_id=1, source_target_pairs={{4,0},{8,4},{12,8},{5,1},{9,5},{13,9},{6,2},{10,6},{14,10},{7,3},{... | collective-permute-start | bytes 3080 | tf_op jit(solution)/shard_map/ppermute | solution.py:34
  27.6 12.1 %collective-permute-start.8 = (f32[256]{0:T(256)S(1)}, f32[256]{0:T(256)S(1)}, u32[]{:S(2)}, u32[]{:S(2)}) collective-permute-start(f32[256]{0:T(256)S(1)} %fusion.278), channel_id=1, source_target_pairs={{0,4},{4,8},{8,12},{1,5},{5,9},{9,13},{2,6},{6,10},{10,14},{3,7},{... | collective-permute-start | bytes 3080 | tf_op jit(solution)/shard_map/ppermute | solution.py:34
  33.2 18.6 %collective-permute-start.2 = (bf16[256,1,258]{0,2,1:T(8,128)(2,1)}, bf16[256,1,258]{0,2,1:T(8,128)(2,1)S(1)}, u32[]{:S(2)}, u32[]{:S(2)}) collective-permute-start(bf16[256,1,258]{0,2,1:T(8,128)(2,1)} %get-tuple-element.26), channel_id=1, source_target_pairs={{0,4},{4,8},{8,12},{1,5},{5,9},{9,13},{2,6},{6,10},{10,14},{3,7},{... | collective-permute-start | bytes 396296 | tf_op jit(solution)/shard_map/ppermute | solution.py:23
  37.2 14.7 %collective-permute-start.3 = (bf16[256,1,258]{0,2,1:T(8,128)(2,1)}, bf16[256,1,258]{0,2,1:T(8,128)(2,1)}, u32[]{:S(2)}, u32[]{:S(2)}) collective-permute-start(bf16[256,1,258]{0,2,1:T(8,128)(2,1)} %get-tuple-element.27), channel_id=1, source_target_pairs={{4,0},{8,4},{12,8},{5,1},{9,5},{13,9},{6,2},{10,6},{14,10},{7,3},{... | collective-permute-start | bytes 396296 | tf_op jit(solution)/shard_map/ppermute | solution.py:26
  38.5 7.8 %collective-permute-start.11 = (f32[256]{0:T(256)S(1)}, f32[256]{0:T(256)S(1)}, u32[]{:S(2)}, u32[]{:S(2)}) collective-permute-start(f32[256]{0:T(256)S(1)} %collective-permute-done.10), channel_id=1, source_target_pairs={{4,0},{8,4},{12,8},{5,1},{9,5},{13,9},{6,2},{10,6},{14,10},{7,3},{... | collective-permute-start | bytes 3080 | tf_op jit(solution)/shard_map/ppermute | solution.py:34
  39.8 6.5 %collective-permute-start.9 = (f32[256]{0:T(256)S(1)}, f32[256]{0:T(256)S(1)}, u32[]{:S(2)}, u32[]{:S(2)}) collective-permute-start(f32[256]{0:T(256)S(1)} %collective-permute-done.8), channel_id=1, source_target_pairs={{0,4},{4,8},{8,12},{1,5},{5,9},{9,13},{2,6},{6,10},{10,14},{3,7},{... | collective-permute-start | bytes 3080 | tf_op jit(solution)/shard_map/ppermute | solution.py:34
  62.1 7.8 %collective-permute-start.17 = (f32[2,256]{1,0:T(2,128)S(1)}, f32[2,256]{1,0:T(2,128)S(1)}, u32[]{:S(2)}, u32[]{:S(2)}) collective-permute-start(f32[2,256]{1,0:T(2,128)S(1)} %rev.13), channel_id=1, source_target_pairs={{4,0},{8,4},{12,8},{5,1},{9,5},{13,9},{6,2},{10,6},{14,10},{7,3},{... | collective-permute-start | bytes 6152 | tf_op jit(solution)/shard_map/ppermute | solution.py:34
  63.4 7.8 %collective-permute-start.16 = (f32[2,256]{1,0:T(2,128)S(1)}, f32[2,256]{1,0:T(2,128)S(1)}, u32[]{:S(2)}, u32[]{:S(2)}) collective-permute-start(f32[2,256]{1,0:T(2,128)S(1)} %slice.463), channel_id=1, source_target_pairs={{0,4},{4,8},{8,12},{1,5},{5,9},{9,13},{2,6},{6,10},{10,14},{3,7},{... | collective-permute-start | bytes 6152 | tf_op jit(solution)/shard_map/ppermute | solution.py:34
  69.9 7.9 %collective-permute-start.19 = (f32[1,256]{1,0:T(1,128)S(1)}, f32[1,256]{1,0:T(1,128)S(1)}, u32[]{:S(2)}, u32[]{:S(2)}) collective-permute-start(f32[1,256]{1,0:T(1,128)S(1)} %get-tuple-element.55), channel_id=1, source_target_pairs={{4,0},{8,4},{12,8},{5,1},{9,5},{13,9},{6,2},{10,6},{14,10},{7,3},{... | collective-permute-start | bytes 3080 | tf_op jit(solution)/shard_map/ppermute | solution.py:34
  71.2 6.6 %collective-permute-start.18 = (f32[1,256]{1,0:T(1,128)S(1)}, f32[1,256]{1,0:T(1,128)S(1)}, u32[]{:S(2)}, u32[]{:S(2)}) collective-permute-start(f32[1,256]{1,0:T(1,128)S(1)} %get-tuple-element.53), channel_id=1, source_target_pairs={{0,4},{4,8},{8,12},{1,5},{5,9},{9,13},{2,6},{6,10},{10,14},{3,7},{... | collective-permute-start | bytes 3080 | tf_op jit(solution)/shard_map/ppermute | solution.py:34
  76.1 7.9 %collective-permute-start.12 = (bf16[256,4,1]{0,2,1:T(2,128)(2,1)S(1)}, bf16[256,4,1]{0,2,1:T(2,128)(2,1)S(1)}, u32[]{:S(2)}, u32[]{:S(2)}) collective-permute-start(bf16[256,4,1]{0,2,1:T(2,128)(2,1)S(1)} %get-tuple-element.32), channel_id=1, source_target_pairs={{0,1},{1,2},{2,3},{3,0},{4,5},{5,6},{6,7},{7,4},{8,9},{9,10},{10,1... | collective-permute-start | bytes 6152 | tf_op jit(solution)/shard_map/ppermute | solution.py:23
  76.1 7.8 %collective-permute-start.13 = (bf16[256,4,1]{0,2,1:T(2,128)(2,1)S(1)}, bf16[256,4,1]{0,2,1:T(2,128)(2,1)S(1)}, u32[]{:S(2)}, u32[]{:S(2)}) collective-permute-start(bf16[256,4,1]{0,2,1:T(2,128)(2,1)S(1)} %get-tuple-element.33), channel_id=1, source_target_pairs={{1,0},{2,1},{3,2},{0,3},{5,4},{6,5},{7,6},{4,7},{9,8},{10,9},{11,1... | collective-permute-start | bytes 6152 | tf_op jit(solution)/shard_map/ppermute | solution.py:26
  77.9 12.1 %collective-permute-start.22 = (f32[256]{0:T(256)S(1)}, f32[256]{0:T(256)S(1)}, u32[]{:S(2)}, u32[]{:S(2)}) collective-permute-start(f32[256]{0:T(256)S(1)} %fusion.274), channel_id=1, source_target_pairs={{4,0},{8,4},{12,8},{5,1},{9,5},{13,9},{6,2},{10,6},{14,10},{7,3},{... | collective-permute-start | bytes 3080 | tf_op jit(solution)/shard_map/ppermute | solution.py:34
  79.2 12.1 %collective-permute-start.20 = (f32[256]{0:T(256)S(1)}, f32[256]{0:T(256)S(1)}, u32[]{:S(2)}, u32[]{:S(2)}) collective-permute-start(f32[256]{0:T(256)S(1)} %fusion.274), channel_id=1, source_target_pairs={{0,4},{4,8},{8,12},{1,5},{5,9},{9,13},{2,6},{6,10},{10,14},{3,7},{... | collective-permute-start | bytes 3080 | tf_op jit(solution)/shard_map/ppermute | solution.py:34
  84.7 17.7 %collective-permute-start.14 = (bf16[256,1,258]{0,2,1:T(8,128)(2,1)}, bf16[256,1,258]{0,2,1:T(8,128)(2,1)S(1)}, u32[]{:S(2)}, u32[]{:S(2)}) collective-permute-start(bf16[256,1,258]{0,2,1:T(8,128)(2,1)} %get-tuple-element.22), channel_id=1, source_target_pairs={{0,4},{4,8},{8,12},{1,5},{5,9},{9,13},{2,6},{6,10},{10,14},{3,7},{... | collective-permute-start | bytes 396296 | tf_op jit(solution)/shard_map/ppermute | solution.py:23
  88.6 13.8 %collective-permute-start.15 = (bf16[256,1,258]{0,2,1:T(8,128)(2,1)}, bf16[256,1,258]{0,2,1:T(8,128)(2,1)}, u32[]{:S(2)}, u32[]{:S(2)}) collective-permute-start(bf16[256,1,258]{0,2,1:T(8,128)(2,1)} %get-tuple-element.23), channel_id=1, source_target_pairs={{4,0},{8,4},{12,8},{5,1},{9,5},{13,9},{6,2},{10,6},{14,10},{7,3},{... | collective-permute-start | bytes 396296 | tf_op jit(solution)/shard_map/ppermute | solution.py:26
  89.9 7.8 %collective-permute-start.23 = (f32[256]{0:T(256)S(1)}, f32[256]{0:T(256)S(1)}, u32[]{:S(2)}, u32[]{:S(2)}) collective-permute-start(f32[256]{0:T(256)S(1)} %collective-permute-done.22), channel_id=1, source_target_pairs={{4,0},{8,4},{12,8},{5,1},{9,5},{13,9},{6,2},{10,6},{14,10},{7,3},{... | collective-permute-start | bytes 3080 | tf_op jit(solution)/shard_map/ppermute | solution.py:34
  91.3 6.5 %collective-permute-start.21 = (f32[256]{0:T(256)S(1)}, f32[256]{0:T(256)S(1)}, u32[]{:S(2)}, u32[]{:S(2)}) collective-permute-start(f32[256]{0:T(256)S(1)} %collective-permute-done.20), channel_id=1, source_target_pairs={{0,4},{4,8},{8,12},{1,5},{5,9},{9,13},{2,6},{6,10},{10,14},{3,7},{... | collective-permute-start | bytes 3080 | tf_op jit(solution)/shard_map/ppermute | solution.py:34
  112.8 7.8 %collective-permute-start.29 = (f32[2,256]{1,0:T(2,128)S(1)}, f32[2,256]{1,0:T(2,128)S(1)}, u32[]{:S(2)}, u32[]{:S(2)}) collective-permute-start(f32[2,256]{1,0:T(2,128)S(1)} %rev.14), channel_id=1, source_target_pairs={{4,0},{8,4},{12,8},{5,1},{9,5},{13,9},{6,2},{10,6},{14,10},{7,3},{... | collective-permute-start | bytes 6152 | tf_op jit(solution)/shard_map/ppermute | solution.py:34
  114.1 7.8 %collective-permute-start.28 = (f32[2,256]{1,0:T(2,128)S(1)}, f32[2,256]{1,0:T(2,128)S(1)}, u32[]{:S(2)}, u32[]{:S(2)}) collective-permute-start(f32[2,256]{1,0:T(2,128)S(1)} %slice.485), channel_id=1, source_target_pairs={{0,4},{4,8},{8,12},{1,5},{5,9},{9,13},{2,6},{6,10},{10,14},{3,7},{... | collective-permute-start | bytes 6152 | tf_op jit(solution)/shard_map/ppermute | solution.py:34
  120.6 7.9 %collective-permute-start.31 = (f32[1,256]{1,0:T(1,128)S(1)}, f32[1,256]{1,0:T(1,128)S(1)}, u32[]{:S(2)}, u32[]{:S(2)}) collective-permute-start(f32[1,256]{1,0:T(1,128)S(1)} %get-tuple-element.51), channel_id=1, source_target_pairs={{4,0},{8,4},{12,8},{5,1},{9,5},{13,9},{6,2},{10,6},{14,10},{7,3},{... | collective-permute-start | bytes 3080 | tf_op jit(solution)/shard_map/ppermute | solution.py:34
  121.9 6.6 %collective-permute-start.30 = (f32[1,256]{1,0:T(1,128)S(1)}, f32[1,256]{1,0:T(1,128)S(1)}, u32[]{:S(2)}, u32[]{:S(2)}) collective-permute-start(f32[1,256]{1,0:T(1,128)S(1)} %get-tuple-element.49), channel_id=1, source_target_pairs={{0,4},{4,8},{8,12},{1,5},{5,9},{9,13},{2,6},{6,10},{10,14},{3,7},{... | collective-permute-start | bytes 3080 | tf_op jit(solution)/shard_map/ppermute | solution.py:34
  126.7 7.7 %collective-permute-start.24 = (bf16[256,4,1]{0,2,1:T(2,128)(2,1)S(1)}, bf16[256,4,1]{0,2,1:T(2,128)(2,1)S(1)}, u32[]{:S(2)}, u32[]{:S(2)}) collective-permute-start(bf16[256,4,1]{0,2,1:T(2,128)(2,1)S(1)} %get-tuple-element.30), channel_id=1, source_target_pairs={{0,1},{1,2},{2,3},{3,0},{4,5},{5,6},{6,7},{7,4},{8,9},{9,10},{10,1... | collective-permute-start | bytes 6152 | tf_op jit(solution)/shard_map/ppermute | solution.py:23
  126.8 7.6 %collective-permute-start.25 = (bf16[256,4,1]{0,2,1:T(2,128)(2,1)S(1)}, bf16[256,4,1]{0,2,1:T(2,128)(2,1)S(1)}, u32[]{:S(2)}, u32[]{:S(2)}) collective-permute-start(bf16[256,4,1]{0,2,1:T(2,128)(2,1)S(1)} %get-tuple-element.31), channel_id=1, source_target_pairs={{1,0},{2,1},{3,2},{0,3},{5,4},{6,5},{7,6},{4,7},{9,8},{10,9},{11,1... | collective-permute-start | bytes 6152 | tf_op jit(solution)/shard_map/ppermute | solution.py:26
  128.5 11.9 %collective-permute-start.34 = (f32[256]{0:T(256)S(1)}, f32[256]{0:T(256)S(1)}, u32[]{:S(2)}, u32[]{:S(2)}) collective-permute-start(f32[256]{0:T(256)S(1)} %fusion.270), channel_id=1, source_target_pairs={{4,0},{8,4},{12,8},{5,1},{9,5},{13,9},{6,2},{10,6},{14,10},{7,3},{... | collective-permute-start | bytes 3080 | tf_op jit(solution)/shard_map/ppermute | solution.py:34
  129.8 11.9 %collective-permute-start.32 = (f32[256]{0:T(256)S(1)}, f32[256]{0:T(256)S(1)}, u32[]{:S(2)}, u32[]{:S(2)}) collective-permute-start(f32[256]{0:T(256)S(1)} %fusion.270), channel_id=1, source_target_pairs={{0,4},{4,8},{8,12},{1,5},{5,9},{9,13},{2,6},{6,10},{10,14},{3,7},{... | collective-permute-start | bytes 3080 | tf_op jit(solution)/shard_map/ppermute | solution.py:34
  135.2 17.9 %collective-permute-start.26 = (bf16[256,1,258]{0,2,1:T(8,128)(2,1)}, bf16[256,1,258]{0,2,1:T(8,128)(2,1)S(1)}, u32[]{:S(2)}, u32[]{:S(2)}) collective-permute-start(bf16[256,1,258]{0,2,1:T(8,128)(2,1)} %get-tuple-element.18), channel_id=1, source_target_pairs={{0,4},{4,8},{8,12},{1,5},{5,9},{9,13},{2,6},{6,10},{10,14},{3,7},{... | collective-permute-start | bytes 396296 | tf_op jit(solution)/shard_map/ppermute | solution.py:23
  139.1 14.0 %collective-permute-start.27 = (bf16[256,1,258]{0,2,1:T(8,128)(2,1)}, bf16[256,1,258]{0,2,1:T(8,128)(2,1)}, u32[]{:S(2)}, u32[]{:S(2)}) collective-permute-start(bf16[256,1,258]{0,2,1:T(8,128)(2,1)} %get-tuple-element.19), channel_id=1, source_target_pairs={{4,0},{8,4},{12,8},{5,1},{9,5},{13,9},{6,2},{10,6},{14,10},{7,3},{... | collective-permute-start | bytes 396296 | tf_op jit(solution)/shard_map/ppermute | solution.py:26
  140.4 7.8 %collective-permute-start.35 = (f32[256]{0:T(256)S(1)}, f32[256]{0:T(256)S(1)}, u32[]{:S(2)}, u32[]{:S(2)}) collective-permute-start(f32[256]{0:T(256)S(1)} %collective-permute-done.34), channel_id=1, source_target_pairs={{4,0},{8,4},{12,8},{5,1},{9,5},{13,9},{6,2},{10,6},{14,10},{7,3},{... | collective-permute-start | bytes 3080 | tf_op jit(solution)/shard_map/ppermute | solution.py:34
  141.7 6.5 %collective-permute-start.33 = (f32[256]{0:T(256)S(1)}, f32[256]{0:T(256)S(1)}, u32[]{:S(2)}, u32[]{:S(2)}) collective-permute-start(f32[256]{0:T(256)S(1)} %collective-permute-done.32), channel_id=1, source_target_pairs={{0,4},{4,8},{8,12},{1,5},{5,9},{9,13},{2,6},{6,10},{10,14},{3,7},{... | collective-permute-start | bytes 3080 | tf_op jit(solution)/shard_map/ppermute | solution.py:34
  163.4 7.8 %collective-permute-start.41 = (f32[2,256]{1,0:T(2,128)S(1)}, f32[2,256]{1,0:T(2,128)S(1)}, u32[]{:S(2)}, u32[]{:S(2)}) collective-permute-start(f32[2,256]{1,0:T(2,128)S(1)} %rev.15), channel_id=1, source_target_pairs={{4,0},{8,4},{12,8},{5,1},{9,5},{13,9},{6,2},{10,6},{14,10},{7,3},{... | collective-permute-start | bytes 6152 | tf_op jit(solution)/shard_map/ppermute | solution.py:34
  164.7 7.8 %collective-permute-start.40 = (f32[2,256]{1,0:T(2,128)S(1)}, f32[2,256]{1,0:T(2,128)S(1)}, u32[]{:S(2)}, u32[]{:S(2)}) collective-permute-start(f32[2,256]{1,0:T(2,128)S(1)} %slice.507), channel_id=1, source_target_pairs={{0,4},{4,8},{8,12},{1,5},{5,9},{9,13},{2,6},{6,10},{10,14},{3,7},{... | collective-permute-start | bytes 6152 | tf_op jit(solution)/shard_map/ppermute | solution.py:34
  171.2 7.9 %collective-permute-start.43 = (f32[1,256]{1,0:T(1,128)S(1)}, f32[1,256]{1,0:T(1,128)S(1)}, u32[]{:S(2)}, u32[]{:S(2)}) collective-permute-start(f32[1,256]{1,0:T(1,128)S(1)} %get-tuple-element.47), channel_id=1, source_target_pairs={{4,0},{8,4},{12,8},{5,1},{9,5},{13,9},{6,2},{10,6},{14,10},{7,3},{... | collective-permute-start | bytes 3080 | tf_op jit(solution)/shard_map/ppermute | solution.py:34
  172.5 6.6 %collective-permute-start.42 = (f32[1,256]{1,0:T(1,128)S(1)}, f32[1,256]{1,0:T(1,128)S(1)}, u32[]{:S(2)}, u32[]{:S(2)}) collective-permute-start(f32[1,256]{1,0:T(1,128)S(1)} %get-tuple-element.45), channel_id=1, source_target_pairs={{0,4},{4,8},{8,12},{1,5},{5,9},{9,13},{2,6},{6,10},{10,14},{3,7},{... | collective-permute-start | bytes 3080 | tf_op jit(solution)/shard_map/ppermute | solution.py:34
  177.4 7.7 %collective-permute-start.36 = (bf16[256,4,1]{0,2,1:T(2,128)(2,1)S(1)}, bf16[256,4,1]{0,2,1:T(2,128)(2,1)S(1)}, u32[]{:S(2)}, u32[]{:S(2)}) collective-permute-start(bf16[256,4,1]{0,2,1:T(2,128)(2,1)S(1)} %get-tuple-element.28), channel_id=1, source_target_pairs={{0,1},{1,2},{2,3},{3,0},{4,5},{5,6},{6,7},{7,4},{8,9},{9,10},{10,1... | collective-permute-start | bytes 6152 | tf_op jit(solution)/shard_map/ppermute | solution.py:23
  177.4 7.6 %collective-permute-start.37 = (bf16[256,4,1]{0,2,1:T(2,128)(2,1)S(1)}, bf16[256,4,1]{0,2,1:T(2,128)(2,1)S(1)}, u32[]{:S(2)}, u32[]{:S(2)}) collective-permute-start(bf16[256,4,1]{0,2,1:T(2,128)(2,1)S(1)} %get-tuple-element.29), channel_id=1, source_target_pairs={{1,0},{2,1},{3,2},{0,3},{5,4},{6,5},{7,6},{4,7},{9,8},{10,9},{11,1... | collective-permute-start | bytes 6152 | tf_op jit(solution)/shard_map/ppermute | solution.py:26
  179.2 11.9 %collective-permute-start.46 = (f32[256]{0:T(256)S(1)}, f32[256]{0:T(256)S(1)}, u32[]{:S(2)}, u32[]{:S(2)}) collective-permute-start(f32[256]{0:T(256)S(1)} %fusion.266), channel_id=1, source_target_pairs={{4,0},{8,4},{12,8},{5,1},{9,5},{13,9},{6,2},{10,6},{14,10},{7,3},{... | collective-permute-start | bytes 3080 | tf_op jit(solution)/shard_map/ppermute | solution.py:34
  180.5 11.9 %collective-permute-start.44 = (f32[256]{0:T(256)S(1)}, f32[256]{0:T(256)S(1)}, u32[]{:S(2)}, u32[]{:S(2)}) collective-permute-start(f32[256]{0:T(256)S(1)} %fusion.266), channel_id=1, source_target_pairs={{0,4},{4,8},{8,12},{1,5},{5,9},{9,13},{2,6},{6,10},{10,14},{3,7},{... | collective-permute-start | bytes 3080 | tf_op jit(solution)/shard_map/ppermute | solution.py:34
  185.8 17.7 %collective-permute-start.38 = (bf16[256,1,258]{0,2,1:T(8,128)(2,1)}, bf16[256,1,258]{0,2,1:T(8,128)(2,1)S(1)}, u32[]{:S(2)}, u32[]{:S(2)}) collective-permute-start(bf16[256,1,258]{0,2,1:T(8,128)(2,1)} %get-tuple-element.14), channel_id=1, source_target_pairs={{0,4},{4,8},{8,12},{1,5},{5,9},{9,13},{2,6},{6,10},{10,14},{3,7},{... | collective-permute-start | bytes 396296 | tf_op jit(solution)/shard_map/ppermute | solution.py:23
  189.8 13.8 %collective-permute-start.39 = (bf16[256,1,258]{0,2,1:T(8,128)(2,1)}, bf16[256,1,258]{0,2,1:T(8,128)(2,1)}, u32[]{:S(2)}, u32[]{:S(2)}) collective-permute-start(bf16[256,1,258]{0,2,1:T(8,128)(2,1)} %get-tuple-element.15), channel_id=1, source_target_pairs={{4,0},{8,4},{12,8},{5,1},{9,5},{13,9},{6,2},{10,6},{14,10},{7,3},{... | collective-permute-start | bytes 396296 | tf_op jit(solution)/shard_map/ppermute | solution.py:26
  191.1 7.8 %collective-permute-start.47 = (f32[256]{0:T(256)S(1)}, f32[256]{0:T(256)S(1)}, u32[]{:S(2)}, u32[]{:S(2)}) collective-permute-start(f32[256]{0:T(256)S(1)} %collective-permute-done.46), channel_id=1, source_target_pairs={{4,0},{8,4},{12,8},{5,1},{9,5},{13,9},{6,2},{10,6},{14,10},{7,3},{... | collective-permute-start | bytes 3080 | tf_op jit(solution)/shard_map/ppermute | solution.py:34
  192.4 6.5 %collective-permute-start.45 = (f32[256]{0:T(256)S(1)}, f32[256]{0:T(256)S(1)}, u32[]{:S(2)}, u32[]{:S(2)}) collective-permute-start(f32[256]{0:T(256)S(1)} %collective-permute-done.44), channel_id=1, source_target_pairs={{0,4},{4,8},{8,12},{1,5},{5,9},{9,13},{2,6},{6,10},{10,14},{3,7},{... | collective-permute-start | bytes 3080 | tf_op jit(solution)/shard_map/ppermute | solution.py:34
  (33 other events, 109.3 us)
where the time goes:
time: 212 us; the launch traced here: 210 us
  starting transfers between devices  127 us (60%)
  local copies, waits for them, and re-layouts  27.6 us (13%)
  other arithmetic  26.9 us (13%)
  matrix products  24.3 us (11%)
  between operations  2.84 us (1%)
    ppermute x32, starting transfers between devices, from_behind(): return lax.ppermute(block, axis, route)  99 us
    dot_general x36, matrix products, apply_taps(): jnp.einsum('co,chw->ohw', kernel[tap_index], window, preferred_element_ty...  20.6 us
    ppermute x8, starting transfers between devices, with_halo(): lax.ppermute(lax.slice_in_dim(block, block.shape[dim] - width, None, axis...  15.9 us
    ppermute x8, starting transfers between devices, with_halo(): lax.ppermute(lax.slice_in_dim(block, 0, width, axis=dim), axis, backward)  12.1 us
    scatter-add x4, other arithmetic, evaluate(): jnp.zeros((current.size,), jnp.float32).at[entry_cell].add(weights * back)  8.27 us
    unnamed x71, local copies, waits for them, and re-layouts  8.15 us
    scatter-add x4, other arithmetic, evaluate(): jnp.zeros(((2 * REACH + 1) * stations,), jnp.float32).at[near_index]  8.12 us
    gather x4, local copies, waits for them, and re-layouts, evaluate(): back = jnp.stack(pieces).reshape(-1)[near_index]  6.89 us
  transfers between devices with their start and end apart: 48, of which 1 were waited for; matrix products, arithmetic and copies ran while one was open for 17% of the time, Pallas kernels for 0%

commit v1 on v0

v1 whole, which is shorter than its diff:
```python
import functools
import math

import jax
import jax.numpy as jnp
from jax import lax
from jax.experimental import pallas as pl
from jax.experimental.pallas import tpu as pltpu
from jax.sharding import PartitionSpec as P

REACH = 2
SPAN = 2 * REACH
noise_levels = (1.0, 0.6, 0.3)
obs_precision = 4.0
step_factor = 0.1

F32 = jnp.float32
BF16 = jnp.bfloat16


def step_table():
    rows = []
    for section in range(2):
        upper = noise_levels[section]
        lower = noise_levels[section + 1]
        spread = upper * upper - lower * lower
        rows.append((upper, spread, math.sqrt(spread)))
        factor = step_factor * lower * lower
        rows.append((lower, factor, math.sqrt(2.0 * factor)))
    return rows


def choose(k, values):
    picked = F32(values[-1])
    for i in range(len(values) - 1):
        picked = jnp.where(k == i, F32(values[i]), picked)
    return picked


def nn(a, b):
    return lax.dot_general(a, b, (((1,), (0,)), ((), ())), preferred_element_type=F32)


def nt(a, b):
    return lax.dot_general(a, b, (((1,), (1,)), ((), ())), preferred_element_type=F32)


def halves(a):
    high = a.astype(BF16)
    low = (a - high.astype(F32)).astype(BF16)
    return high, low


def silu_rms(values, half_gain):
    power = jnp.mean(values * values, axis=0, keepdims=True)
    h = values * lax.rsqrt(power + 1e-06) * half_gain
    return h + h * jnp.tanh(h)


def kernel(
    nb, nw, rows, nv, nc, lon,
    x0, noise, sv, cell, owner, slot, weight, live, lift, conv, head, g1, g2,
    out, innov,
    x, sc, lifted, act, onehot, slothot, wmask, offmask,
    tsend, psend, rowbuf, tilebuf, partbuf,
    send_sem, recv_sem,
):
    me = lax.axis_index("band")
    col = lax.axis_index("wt")
    left = lax.rem(col + nw - 1, nw)
    right = lax.rem(col + 1, nw)
    dists = [d for d in range(-SPAN, SPAN + 1) if d != 0 and abs(d) < nb]

    def exists(d):
        return jnp.logical_and(me + d >= 0, me + d < nb)

    rowbuf[...] = jnp.zeros_like(rowbuf)
    tilebuf[...] = jnp.zeros_like(tilebuf)
    partbuf[...] = jnp.zeros_like(partbuf)

    barrier = pltpu.get_barrier_semaphore()

    def greet(b, w):
        pl.semaphore_signal(
            barrier, inc=1, device_id={"band": b, "wt": w}, device_id_type=pl.DeviceIdType.MESH
        )

    greet(me, left)
    greet(me, right)
    for d in dists:
        @pl.when(exists(d))
        def _():
            greet(me + d, col)
            if abs(d) == 1:
                greet(me + d, left)
                greet(me + d, right)

    e = cell.shape[1]
    c = cell[...]
    alive = lax.broadcasted_iota(jnp.int32, (1, e), 1) < live[0]
    weights = jnp.where(alive, weight[...], F32(0.0))
    var = c // (rows * lon)
    rest = c - var * (rows * lon)
    rowof = rest // lon
    lonof = rest - rowof * lon
    target = rowof * nv + var
    first_iota = lax.broadcasted_iota(jnp.int32, (lon, e), 0)
    onehot[...] = jnp.where(first_iota == lonof, F32(1.0), F32(0.0)).astype(BF16)
    slothot[...] = jnp.where(
        lax.broadcasted_iota(jnp.int32, (sv.shape[1], e), 0) == slot[...], F32(1.0), F32(0.0)
    ).astype(BF16)
    wmask[...] = jnp.where(
        lax.broadcasted_iota(jnp.int32, (rows * nv, e), 0) == target, weights, F32(0.0)
    )
    offset = owner[...] - me + REACH
    offmask[...] = jnp.where(
        lax.broadcasted_iota(jnp.int32, (8, e), 0) == offset, F32(1.0), F32(0.0)
    )
    x[...] = x0[...]

    peers = 2
    for d in dists:
        peers = peers + jnp.where(exists(d), 3 if abs(d) == 1 else 1, 0)
    pl.semaphore_wait(barrier, peers)

    lane = lax.broadcasted_iota(jnp.int32, (1, 128), 1)
    row8 = lax.broadcasted_iota(jnp.int32, (8, 1), 0)
    table = step_table()

    def step(k, carry):
        inverse = choose(k, [1.0 / math.sqrt(1.0 + r[0] * r[0]) for r in table])
        score_factor = choose(k, [r[1] / r[0] for r in table])
        adjoint_factor = choose(k, [obs_precision * r[1] for r in table])
        noise_factor = choose(k, [r[2] for r in table])

        def remote(index, source, target_ref, b, w):
            return pltpu.make_async_remote_copy(
                src_ref=source, dst_ref=target_ref,
                send_sem=send_sem.at[index], recv_sem=recv_sem.at[k, index],
                device_id={"band": b, "wt": w}, device_id_type=pl.DeviceIdType.MESH,
            )

        copies = [
            (None, remote(0, tsend, tilebuf.at[k, 0], me, right)),
            (None, remote(1, tsend, tilebuf.at[k, 1], me, left)),
            (1, remote(2, sc.at[rows - 1], rowbuf.at[k, 0], me + 1, col)),
            (-1, remote(3, sc.at[0], rowbuf.at[k, 1], me - 1, col)),
            (1, remote(4, tsend, tilebuf.at[k, 2], me + 1, right)),
            (1, remote(5, tsend, tilebuf.at[k, 3], me + 1, left)),
            (-1, remote(6, tsend, tilebuf.at[k, 4], me - 1, right)),
            (-1, remote(7, tsend, tilebuf.at[k, 5], me - 1, left)),
        ]
        parts = [
            (d, remote(8 + i, psend, partbuf.at[k, SPAN - d], me + d, col))
            for i, d in enumerate(dists)
        ]

        def when(d, f):
            if d is None:
                f()
            else:
                pl.when(exists(d))(f)

        tile = jnp.zeros((nv, 128), F32)
        for r in range(rows):
            s = x[pl.ds(r * nv, nv), :] * inverse
            sc[r] = s.astype(BF16)
            tail = pltpu.roll(s[:, lon - 128:], 2 * r + 3, 1)
            start = pltpu.roll(s[:, :128], 2 * r + 1, 1)
            tile = jnp.where(lane == 2 * r + 2, tail, tile)
            tile = jnp.where(lane == 2 * r + 1, start, tile)
        tsend[...] = tile.astype(BF16)
        for d, copy in copies:
            when(d, copy.start)

        high, low = halves(x[...])
        hot = onehot[...]
        picked = nn(high, hot) + nn(low, hot)
        values = jnp.sum(picked * wmask[...], axis=0, keepdims=True)
        high, low = halves(values * offmask[...])
        part = nt(high, slothot[...]) + nt(low, slothot[...])
        psend[...] = jnp.where(row8 == 2 * REACH + 1, sv[...], part)
        for d, copy in parts:
            when(d, copy.start)

        def widen(r, f):
            act[r, 1] = f.astype(BF16)
            near, far = f[:, :128], f[:, lon - 128:]
            a0, a1 = pltpu.roll(near, 1, 1), pltpu.roll(far, 1, 1)
            b0, b1 = pltpu.roll(near, 127, 1), pltpu.roll(far, 127, 1)
            act[r, 0, :, :128] = a0.astype(BF16)
            act[r, 0, :, 128:] = jnp.where(lane == 0, a0, a1).astype(BF16)
            act[r, 2, :, :128] = jnp.where(lane == 127, b1, b0).astype(BF16)
            act[r, 2, :, 128:] = b1.astype(BF16)

        half1 = g1[...]
        wide1 = jnp.concatenate([half1, half1], axis=1)
        for r in range(rows):
            v = nn(lift[...], sc[r])
            lifted[r] = v
            widen(r + 1, silu_rms(v, wide1))

        for d, copy in copies:
            when(None if d is None else -d, copy.wait_recv)
        for r, i in ((0, 0), (rows + 1, 1)):
            widen(r, silu_rms(nn(lift[...], rowbuf[k, i]), wide1))
        t = [tilebuf[k, i].astype(F32) for i in range(6)]
        edge = jnp.where(lane == 0, pltpu.roll(t[2], 128 - 2 * rows, 1), F32(0.0))
        edge = jnp.where(lane == 127, pltpu.roll(t[3], 128 - 2 * rows, 1), edge)
        inner = jnp.logical_and(lane >= 1, lane <= 2 * rows)
        even = lane % 2 == 0
        edge = jnp.where(jnp.logical_and(inner, even), t[0], edge)
        edge = jnp.where(jnp.logical_and(inner, jnp.logical_not(even)), t[1], edge)
        edge = jnp.where(lane == 2 * rows + 2, pltpu.roll(t[4], 2 * rows, 1), edge)
        edge = jnp.where(lane == 2 * rows + 1, pltpu.roll(t[5], 2 * rows, 1), edge)
        rim = silu_rms(nn(lift[...], edge.astype(BF16)), half1)
        for r in range(rows + 2):
            here = rim if r == 0 else pltpu.roll(rim, 128 - 2 * r, 1)
            now = act[r, 0, :, :128].astype(F32)
            act[r, 0, :, :128] = jnp.where(lane == 0, here, now).astype(BF16)
            now = act[r, 2, :, 128:].astype(F32)
            act[r, 2, :, 128:] = jnp.where(lane == 127, here, now).astype(BF16)

        half2 = g2[...]
        wide2 = jnp.concatenate([half2, half2], axis=1)
        scores = []
        for r in range(rows):
            window = act[pl.ds(r, 3)].reshape(9 * nc, lon)
            mixed = lifted[r] + nn(conv[...], window)
            second = silu_rms(mixed, wide2).astype(BF16)
            scores.append(nn(head[...], second))

        for d, copy in parts:
            when(-d, copy.wait_recv)
        mine = psend[...]
        total = mine
        observed = jnp.where(row8 == REACH, sv[...], F32(0.0))
        for d in dists:
            got = partbuf[k, d + SPAN]
            keep = jnp.logical_and(row8 >= max(0, d), row8 <= min(SPAN, SPAN + d))
            total = total + jnp.where(keep, pltpu.roll(got, d % 8, 0), F32(0.0))
            if abs(d) <= REACH:
                observed = jnp.where(row8 == d + REACH, got[SPAN + 1:SPAN + 2], observed)
        difference = jnp.where(row8 <= SPAN, observed - total, F32(0.0))
        innov[...] = difference[REACH:REACH + 1]
        high, low = halves(difference)
        back = nn(high, slothot[...]) + nn(low, slothot[...])
        back = jnp.sum(back * offmask[...], axis=0, keepdims=True)
        high, low = halves(wmask[...] * back)
        adjoint = nt(high, hot) + nt(low, hot)

        for r in range(rows):
            here = pl.ds(r * nv, nv)
            x[here, :] = (
                x[here, :]
                + score_factor * scores[r]
                + adjoint_factor * adjoint[r * nv:(r + 1) * nv]
                + noise_factor * noise[k, r * nv:(r + 1) * nv, :]
            )
        for d, copy in copies + parts:
            when(d, copy.wait_send)
        return carry

    lax.fori_loop(0, len(table), step, 0)
    out[...] = x[...]


def per_device(
    nb, nw,
    prior_state, langevin_noise, station_values, entry_cell, entry_owner, entry_slot,
    entry_weight, live_counts, lift_weight, conv_weight, head_weight, first_gain, second_gain,
):
    nv, rows, lon = prior_state.shape
    nc = lift_weight.shape[1]
    steps = langevin_noise.shape[0]
    stations = station_values.shape[0]
    e = entry_cell.shape[0]
    x0 = prior_state.transpose(1, 0, 2).reshape(rows * nv, lon)
    noise = langevin_noise.transpose(0, 2, 1, 3).reshape(steps, rows * nv, lon)
    conv = conv_weight.reshape(9 * nc, nc).T
    row = lambda a: a.reshape(1, -1)
    gain = lambda g: jnp.broadcast_to((0.5 * g)[:, None], (nc, 128))
    vmem = pl.BlockSpec(memory_space=pltpu.VMEM)
    count = 8 + 2 * SPAN
    state, innov = pl.pallas_call(
        functools.partial(kernel, nb, nw, rows, nv, nc, lon),
        out_shape=(
            jax.ShapeDtypeStruct((rows * nv, lon), F32),
            jax.ShapeDtypeStruct((1, stations), F32),
        ),
        in_specs=[vmem] * 7 + [pl.BlockSpec(memory_space=pltpu.SMEM)] + [vmem] * 5,
        out_specs=(vmem, vmem),
        scratch_shapes=[
            pltpu.VMEM((rows * nv, lon), F32),
            pltpu.VMEM((rows, nv, lon), BF16),
            pltpu.VMEM((rows, nc, lon), F32),
            pltpu.VMEM((rows + 2, 3, nc, lon), BF16),
            pltpu.VMEM((lon, e), BF16),
            pltpu.VMEM((stations, e), BF16),
            pltpu.VMEM((rows * nv, e), F32),
            pltpu.VMEM((8, e), F32),
            pltpu.VMEM((nv, 128), BF16),
            pltpu.VMEM((8, stations), F32),
            pltpu.VMEM((steps, 2, nv, lon), BF16),
            pltpu.VMEM((steps, 6, nv, 128), BF16),
            pltpu.VMEM((steps, 2 * SPAN + 1, 8, stations), F32),
            pltpu.SemaphoreType.DMA((count,)),
            pltpu.SemaphoreType.DMA((steps, count)),
        ],
        compiler_params=pltpu.CompilerParams(
            collective_id=0, has_side_effects=True, vmem_limit_bytes=40 * 1024 * 1024
        ),
    )(
        x0, noise, row(station_values), row(entry_cell), row(entry_owner), row(entry_slot),
        row(entry_weight), live_counts, lift_weight.T, conv, head_weight.T,
        gain(first_gain), gain(second_gain),
    )
    return state.reshape(rows, nv, lon).transpose(1, 0, 2), innov.reshape(-1)


def solution(mesh):
    ring = ("groups", "band", "wt")
    in_specs = (
        P(*ring), P(None, *ring), P(ring), P(ring), P(ring), P(ring), P(ring), P(ring),
        P(), P(), P(), P(), P(),
    )
    out_specs = (P(*ring), P(ring))
    return jax.shard_map(
        functools.partial(per_device, mesh.shape["band"], mesh.shape["wt"]),
        mesh=mesh, in_specs=in_specs, out_specs=out_specs, check_vma=False,
    )
```

time: 212 us -> 48.7 us (0.23)
  starting transfers between devices: 127 us -> 0 us
  Pallas kernels: 0 us -> 39 us
  other arithmetic: 26.9 us -> 1.36 us
  matrix products: 24.3 us -> 0 us
  local copies, waits for them, and re-layouts: 27.6 us -> 6.54 us
    ppermute x48 -> x0, starting transfers between devices: 127 us -> none  [the longest x32 99 us: from_behind(): return lax.ppermute(block, axis, route)]
    pallas_call x0 -> x1, Pallas kernels: none -> 39 us  [per_device(): pl.pallas_call(functools.partial(kernel, nb, nw, rows, nv, nc, lon), out_...]
    dot_general x44 -> x0, matrix products: 24.3 us -> none  [the longest x36 20.6 us: apply_taps(): jnp.einsum('co,chw->ohw', kernel[tap_index], window, preferred_element_ty...]
    scatter-add x8 -> x0, other arithmetic: 16.4 us -> none  [the longest x4 8.27 us: evaluate(): jnp.zeros((current.size,), jnp.float32).at[entry_cell].add(weights * back)]
    gather x8 -> x0, local copies, waits for them, and re-layouts: 13.8 us -> none  [the longest x4 6.89 us: evaluate(): back = jnp.stack(pieces).reshape(-1)[near_index]]
    unnamed x71 -> x14, local copies, waits for them, and re-layouts: 8.15 us -> 1.47 us
    concatenate x4 -> x0, other arithmetic: 4.24 us -> none  [with_halo(): block = jnp.concatenate([low, block, high], axis=dim)]
    mul x4 -> x0, local copies, waits for them, and re-layouts: 3.53 us -> none  [evaluate(): return (score + obs_precision * adjoint.reshape(current.shape), innov)]
  transfers between devices with their start and end apart: 48 -> 0, of which waited for: 1 -> 0; matrix products, arithmetic and copies ran while one was open for 17% -> 0% of each run, Pallas kernels for 0% -> 0%
where the time goes in v1:
time: 48.7 us; the launch traced here: 48.4 us
  Pallas kernels  39 us (80%)
  local copies, waits for them, and re-layouts  6.54 us (13%)
  between operations  1.41 us (3%)
  other arithmetic  1.36 us (3%)
    pallas_call x1, Pallas kernels, per_device(): pl.pallas_call(functools.partial(kernel, nb, nw, rows, nv, nc, lon), out_...  39 us
    reshape x1, local copies, waits for them, and re-layouts, per_device(): conv = conv_weight.reshape(9 * nc, nc).T  1.59 us
    unnamed x14, local copies, waits for them, and re-layouts  1.47 us
    transpose x1, local copies, waits for them, and re-layouts, per_device(): noise = langevin_noise.transpose(0, 2, 1, 3).reshape(steps, rows * nv, lon)  1.41 us
    mul x2, other arithmetic, per_device(): gain = lambda g: jnp.broadcast_to((0.5 * g)[:, None], (nc, 128))  1.36 us
    transpose x1, local copies, waits for them, and re-layouts, per_device(): x0 = prior_state.transpose(1, 0, 2).reshape(rows * nv, lon)  1.01 us

profile of v1, /device:TPU:0, one launch (start us, length us, event | category | flops | bytes accessed | tf_op | source)
XLA Modules:
  0.0 48.4 jit_solution(7067534875147234980)
XLA Ops:
  1.3 0.7 %broadcast_multiply_fusion.1 = f32[256]{0:T(256)S(1)} fusion(f32[256]{0:T(256)} %param.24), kind=kLoop, calls=%fused_computation.2 | loop fusion | flops 256 | bytes 2048 | tf_op jit(solution)/shard_map/mul | solution.py:282
  2.0 0.7 %broadcast_multiply_fusion = f32[256]{0:T(256)S(1)} fusion(f32[256]{0:T(256)} %param.25), kind=kLoop, calls=%fused_computation.1 | loop fusion | flops 256 | bytes 2048 | tf_op jit(solution)/shard_map/mul | solution.py:282
  2.6 0.9 %copy.22 = bf16[64,256]{0,1:T(8,128)(2,1)S(1)} copy(bf16[64,256]{1,0:T(8,128)(2,1)} %param.21) | data formatting | bytes 65536 | tf_op args[8]
  3.5 0.1 broadcast_in_dim.5.g2
  3.6 0.1 broadcast_in_dim.4.g1
  3.7 1.0 %copy.20 = f32[4,64,256]{2,1,0:T(8,128)S(1)} copy(f32[4,64,256]{2,0,1:T(4,128)} %bitcast.32) | data formatting | bytes 524288 | tf_op jit(solution)/shard_map/transpose | solution.py:278
  4.7 1.4 %copy.21 = f32[4,4,64,256]{3,2,1,0:T(8,128)S(1)} copy(f32[4,4,64,256]{3,1,2,0:T(4,128)} %bitcast.31) | data formatting | bytes 2097152 | tf_op jit(solution)/shard_map/transpose | solution.py:279
  6.1 0.0 copy-start
  6.2 0.0 copy-start.1
  6.2 0.0 copy-start.2
  6.2 0.0 copy-start.3
  6.2 0.0 copy-start.4
  6.2 0.0 copy-start.5
  6.2 1.6 %copy.23 = bf16[2304,256]{0,1:T(8,128)(2,1)S(1)} copy(bf16[2304,256]{1,0:T(8,128)(2,1)} %bitcast.30) | data formatting | bytes 2359296 | tf_op jit(solution)/shard_map/reshape | solution.py:280
  7.8 0.0 copy-done
  7.8 0.0 copy-done.1
  7.8 0.0 copy-done.2
  7.8 0.0 copy-done.3
  7.9 0.0 copy-done.4
  7.9 0.0 copy-done.5
  7.9 39.0 %shard_map.140 = (f32[256,256]{1,0:T(8,128)S(1)}, f32[1,256]{1,0:T(1,128)S(1)}) custom-call(f32[256,256]{1,0:T(8,128)S(1)} %bitcast.20, f32[4,256,256]{2,1,0:T(8,128)S(1)} %bitcast.19, f32[1,256]{1,0:T(1,128)S(1)} %bitcast.24, s32[1,256]{1,0:T(1,128)S(1)} %bitcast.25, s32[1,256]{1,0:T(1,128)S(1)} %bitcast.26, s32[1,256]{1,0:T(1,128)S(1)} %bitcast.27, ...), custom_call_target="tpu_custom_call" | custom-call | tf_op jit(solution)/shard_map/pallas_call | solution.py:285
  46.9 0.9 %copy.26 = f32[4,64,256]{2,0,1:T(4,128)} copy(f32[4,64,256]{2,1,0:T(8,128)S(1)} %bitcast.22) | data formatting | bytes 524288 | tf_op jit(solution)/shard_map/reshape | solution.py:318
  47.8 0.6 %copy.29 = f32[256]{0:T(256)} copy(f32[256]{0:T(256)S(1)} %bitcast.29) | data formatting | bytes 2048
Async XLA Ops:
  6.1 1.7 %copy-start = (bf16[256,64]{0,1:T(8,128)(2,1)S(1)}, bf16[256,64]{0,1:T(8,128)(2,1)}, u32[]{:S(2)}) copy-start(bf16[256,64]{0,1:T(8,128)(2,1)} %param.23) | copy-start | bytes 98308
  6.2 1.7 %copy-start.1 = (f32[256]{0:T(256)S(1)}, f32[256]{0:T(256)}, u32[]{:S(2)}) copy-start(f32[256]{0:T(256)} %param.15) | copy-start | bytes 3076
  6.2 1.7 %copy-start.2 = (s32[256]{0:T(256)S(1)}, s32[256]{0:T(256)}, u32[]{:S(2)}) copy-start(s32[256]{0:T(256)} %param.16) | copy-start | bytes 3076
  6.2 1.7 %copy-start.3 = (s32[256]{0:T(256)S(1)}, s32[256]{0:T(256)}, u32[]{:S(2)}) copy-start(s32[256]{0:T(256)} %param.17) | copy-start | bytes 3076
  6.2 1.7 %copy-start.4 = (s32[256]{0:T(256)S(1)}, s32[256]{0:T(256)}, u32[]{:S(2)}) copy-start(s32[256]{0:T(256)} %param.18) | copy-start | bytes 3076
  6.2 1.7 %copy-start.5 = (f32[256]{0:T(256)S(1)}, f32[256]{0:T(256)}, u32[]{:S(2)}) copy-start(f32[256]{0:T(256)} %param.19) | copy-start | bytes 3076

commit v2 on v1

--- a/solution.py
+++ b/solution.py
@@ -59,9 +59,9 @@
 
 def kernel(
     nb, nw, rows, nv, nc, lon,
-    x0, noise, sv, cell, owner, slot, weight, live, lift, conv, head, g1, g2,
+    x0, noise, sv, cell, owner, slot, weight, live, lift_in, conv_in, head, gain1, gain2,
     out, innov,
-    x, sc, lifted, act, onehot, slothot, wmask, offmask,
+    x, lift, conv, g1, g2, sc, lifted, act, onehot, slothot, wmask, offmask,
     tsend, psend, rowbuf, tilebuf, partbuf,
     send_sem, recv_sem,
 ):
@@ -69,6 +69,11 @@
     col = lax.axis_index("wt")
     left = lax.rem(col + nw - 1, nw)
     right = lax.rem(col + 1, nw)
+    sides = lon // 128
+
+    def lines_of(r, h):
+        return pl.ds(h * rows + r, nv, stride=sides * rows)
+
     dists = [d for d in range(-SPAN, SPAN + 1) if d != 0 and abs(d) < nb]
 
     def exists(d):
@@ -116,7 +121,15 @@
     offmask[...] = jnp.where(
         lax.broadcasted_iota(jnp.int32, (8, e), 0) == offset, F32(1.0), F32(0.0)
     )
-    x[...] = x0[...]
+    for r in range(rows):
+        for h in range(sides):
+            x[pl.ds(r * nv, nv), 128 * h:128 * (h + 1)] = x0[lines_of(r, h), :]
+
+    lift[...] = lift_in[...].T
+    for t in range(9):
+        conv[:, t * nc:(t + 1) * nc] = conv_in[t].T
+    g1[...] = jnp.broadcast_to(0.5 * gain1[...], (128, nc)).T
+    g2[...] = jnp.broadcast_to(0.5 * gain2[...], (128, nc)).T
 
     peers = 2
     for d in dists:
@@ -255,14 +268,18 @@
                 x[here, :]
                 + score_factor * scores[r]
                 + adjoint_factor * adjoint[r * nv:(r + 1) * nv]
-                + noise_factor * noise[k, r * nv:(r + 1) * nv, :]
+                + noise_factor * jnp.concatenate(
+                    [noise[k, lines_of(r, h), :] for h in range(sides)], axis=1
+                )
             )
         for d, copy in copies + parts:
             when(d, copy.wait_send)
         return carry
 
     lax.fori_loop(0, len(table), step, 0)
-    out[...] = x[...]
+    for r in range(rows):
+        for h in range(sides):
+            out[lines_of(r, h), :] = x[pl.ds(r * nv, nv), 128 * h:128 * (h + 1)]
 
 
 def per_device(
@@ -275,23 +292,28 @@
     steps = langevin_noise.shape[0]
     stations = station_values.shape[0]
     e = entry_cell.shape[0]
-    x0 = prior_state.transpose(1, 0, 2).reshape(rows * nv, lon)
-    noise = langevin_noise.transpose(0, 2, 1, 3).reshape(steps, rows * nv, lon)
-    conv = conv_weight.reshape(9 * nc, nc).T
+    sides = lon // 128
+    lines = nv * sides * rows
+    x0 = prior_state.reshape(nv, rows, sides, 128).transpose(0, 2, 1, 3).reshape(lines, 128)
+    noise = langevin_noise.reshape(steps, nv, rows, sides, 128)
+    noise = noise.transpose(0, 1, 3, 2, 4).reshape(steps, lines, 128)
     row = lambda a: a.reshape(1, -1)
-    gain = lambda g: jnp.broadcast_to((0.5 * g)[:, None], (nc, 128))
     vmem = pl.BlockSpec(memory_space=pltpu.VMEM)
     count = 8 + 2 * SPAN
     state, innov = pl.pallas_call(
         functools.partial(kernel, nb, nw, rows, nv, nc, lon),
         out_shape=(
-            jax.ShapeDtypeStruct((rows * nv, lon), F32),
+            jax.ShapeDtypeStruct((lines, 128), F32),
             jax.ShapeDtypeStruct((1, stations), F32),
         ),
         in_specs=[vmem] * 7 + [pl.BlockSpec(memory_space=pltpu.SMEM)] + [vmem] * 5,
         out_specs=(vmem, vmem),
         scratch_shapes=[
             pltpu.VMEM((rows * nv, lon), F32),
+            pltpu.VMEM((nc, nv), BF16),
+            pltpu.VMEM((nc, 9 * nc), BF16),
+            pltpu.VMEM((nc, 128), F32),
+            pltpu.VMEM((nc, 128), F32),
             pltpu.VMEM((rows, nv, lon), BF16),
             pltpu.VMEM((rows, nc, lon), F32),
             pltpu.VMEM((rows + 2, 3, nc, lon), BF16),
@@ -312,10 +334,11 @@
         ),
     )(
         x0, noise, row(station_values), row(entry_cell), row(entry_owner), row(entry_slot),
-        row(entry_weight), live_counts, lift_weight.T, conv, head_weight.T,
-        gain(first_gain), gain(second_gain),
-    )
-    return state.reshape(rows, nv, lon).transpose(1, 0, 2), innov.reshape(-1)
+        row(entry_weight), live_counts, lift_weight, conv_weight, head_weight.T,
+        row(first_gain), row(second_gain),
+    )
+    state = state.reshape(nv, sides, rows, 128).transpose(0, 2, 1, 3).reshape(nv, rows, lon)
+    return state, innov.reshape(-1)
 
 
 def solution(mesh):

time: 48.7 us -> 51.8 us (1.064)
  local copies, waits for them, and re-layouts: 6.54 us -> 11 us
  other arithmetic: 1.36 us -> 0 us
    unnamed x14 -> x26, local copies, waits for them, and re-layouts: 1.47 us -> 11 us
    reshape x2 -> x0, local copies, waits for them, and re-layouts: 2.46 us -> none  [the longest x1 1.59 us: per_device(): conv = conv_weight.reshape(9 * nc, nc).T]
    transpose x2 -> x0, local copies, waits for them, and re-layouts: 2.42 us -> none  [the longest x1 1.41 us: per_device(): noise = langevin_noise.transpose(0, 2, 1, 3).reshape(steps, rows * nv, lon)]
    mul x2 -> x0, other arithmetic: 1.36 us -> none  [per_device(): gain = lambda g: jnp.broadcast_to((0.5 * g)[:, None], (nc, 128))]
where the time goes in v2:
time: 51.8 us; the launch traced here: 51.3 us
  Pallas kernels  39 us (75%)
  local copies, waits for them, and re-layouts  11 us (21%)
  between operations  1.31 us (3%)
    pallas_call x1, Pallas kernels, per_device(): pl.pallas_call(functools.partial(kernel, nb, nw, rows, nv, nc, lon), out_...  39 us
    unnamed x26, local copies, waits for them, and re-layouts  11 us

profile of v2, /device:TPU:0, one launch (start us, length us, event | category | flops | bytes accessed | tf_op | source)
XLA Modules:
  0.0 51.3 jit_solution(4738735410820423920)
XLA Ops:
  1.3 0.0 copy-start
  1.3 1.3 %copy-done = bf16[9,256,256]{2,1,0:T(8,128)(2,1)S(1)} copy-done((bf16[9,256,256]{2,1,0:T(8,128)(2,1)S(1)}, bf16[9,256,256]{2,1,0:T(8,128)(2,1)}, u32[]{:S(2)}) %copy-start) | copy-done | bytes 1179672
  2.6 0.0 copy-start.1
  2.6 1.2 %copy-done.1 = f32[4,64,4,256]{3,2,1,0:T(4,128)S(1)} copy-done((f32[4,64,4,256]{3,2,1,0:T(4,128)S(1)}, f32[4,64,4,256]{3,2,1,0:T(4,128)}, u32[]{:S(2)}) %copy-start.1) | copy-done | bytes 1048600
  3.8 0.0 copy-start.2
  3.8 0.9 %copy-done.2 = f32[64,4,256]{2,1,0:T(4,128)S(1)} copy-done((f32[64,4,256]{2,1,0:T(4,128)S(1)}, f32[64,4,256]{2,1,0:T(4,128)}, u32[]{:S(2)}) %copy-start.2) | copy-done | bytes 262168
  4.7 0.0 copy-start.3
  4.7 0.8 %copy-done.3 = bf16[64,256]{1,0:T(8,128)(2,1)S(1)} copy-done((bf16[64,256]{1,0:T(8,128)(2,1)S(1)}, bf16[64,256]{1,0:T(8,128)(2,1)}, u32[]{:S(2)}) %copy-start.3) | copy-done | bytes 32792
  5.5 0.0 copy-start.4
  5.5 0.8 %copy-done.4 = bf16[256,64]{0,1:T(8,128)(2,1)S(1)} copy-done((bf16[256,64]{0,1:T(8,128)(2,1)S(1)}, bf16[256,64]{0,1:T(8,128)(2,1)}, u32[]{:S(2)}) %copy-start.4) | copy-done | bytes 32792
  6.2 0.0 copy-start.5
  6.2 0.7 %copy-done.5 = f32[256]{0:T(256)S(1)} copy-done((f32[256]{0:T(256)S(1)}, f32[256]{0:T(256)}, u32[]{:S(2)}) %copy-start.5) | copy-done | bytes 1048
  6.9 0.0 copy-start.6
  6.9 0.7 %copy-done.6 = s32[256]{0:T(256)S(1)} copy-done((s32[256]{0:T(256)S(1)}, s32[256]{0:T(256)}, u32[]{:S(2)}) %copy-start.6) | copy-done | bytes 1048
  7.6 0.0 copy-start.7
  7.6 0.7 %copy-done.7 = s32[256]{0:T(256)S(1)} copy-done((s32[256]{0:T(256)S(1)}, s32[256]{0:T(256)}, u32[]{:S(2)}) %copy-start.7) | copy-done | bytes 1048
  8.3 0.0 copy-start.8
  8.3 0.7 %copy-done.8 = s32[256]{0:T(256)S(1)} copy-done((s32[256]{0:T(256)S(1)}, s32[256]{0:T(256)}, u32[]{:S(2)}) %copy-start.8) | copy-done | bytes 1048
  9.0 0.0 copy-start.9
  9.0 0.7 %copy-done.9 = f32[256]{0:T(256)S(1)} copy-done((f32[256]{0:T(256)S(1)}, f32[256]{0:T(256)}, u32[]{:S(2)}) %copy-start.9) | copy-done | bytes 1048
  9.6 0.0 copy-start.10
  9.6 0.7 %copy-done.10 = f32[256]{0:T(256)S(1)} copy-done((f32[256]{0:T(256)S(1)}, f32[256]{0:T(256)}, u32[]{:S(2)}) %copy-start.10) | copy-done | bytes 1048
  10.3 0.0 copy-start.11
  10.3 0.7 %copy-done.11 = f32[256]{0:T(256)S(1)} copy-done((f32[256]{0:T(256)S(1)}, f32[256]{0:T(256)}, u32[]{:S(2)}) %copy-start.11) | copy-done | bytes 1048
  11.0 39.0 %shard_map.140 = (f32[512,128]{1,0:T(8,128)S(1)}, f32[1,256]{1,0:T(1,128)S(1)}) custom-call(f32[512,128]{1,0:T(8,128)S(1)} %bitcast.25, f32[4,512,128]{2,1,0:T(8,128)S(1)} %bitcast.24, f32[1,256]{1,0:T(1,128)S(1)} %bitcast.28, s32[1,256]{1,0:T(1,128)S(1)} %bitcast.29, s32[1,256]{1,0:T(1,128)S(1)} %bitcast.30, s32[1,256]{1,0:T(1,128)S(1)} %bitcast.31, ...), custom_call_target="tpu_custom_call" | custom-call | tf_op jit(solution)/shard_map/pallas_call | solution.py:303
  50.0 0.7 %copy.21 = f32[64,4,256]{2,1,0:T(4,128)} copy(f32[64,4,256]{2,1,0:T(4,128)S(1)} %bitcast.26) | data formatting | bytes 524288
  50.7 0.6 %copy.22 = f32[256]{0:T(256)} copy(f32[256]{0:T(256)S(1)} %bitcast.35) | data formatting | bytes 2048
Async XLA Ops:
  1.3 1.3 %copy-start = (bf16[9,256,256]{2,1,0:T(8,128)(2,1)S(1)}, bf16[9,256,256]{2,1,0:T(8,128)(2,1)}, u32[]{:S(2)}) copy-start(bf16[9,256,256]{2,1,0:T(8,128)(2,1)} %conv_in.1) | copy-start | bytes 3538948
  2.6 1.2 %copy-start.1 = (f32[4,64,4,256]{3,2,1,0:T(4,128)S(1)}, f32[4,64,4,256]{3,2,1,0:T(4,128)}, u32[]{:S(2)}) copy-start(f32[4,64,4,256]{3,2,1,0:T(4,128)} %param.14) | copy-start | bytes 3145732
  3.8 0.9 %copy-start.2 = (f32[64,4,256]{2,1,0:T(4,128)S(1)}, f32[64,4,256]{2,1,0:T(4,128)}, u32[]{:S(2)}) copy-start(f32[64,4,256]{2,1,0:T(4,128)} %param.13) | copy-start | bytes 786436
  4.7 0.8 %copy-start.3 = (bf16[64,256]{1,0:T(8,128)(2,1)S(1)}, bf16[64,256]{1,0:T(8,128)(2,1)}, u32[]{:S(2)}) copy-start(bf16[64,256]{1,0:T(8,128)(2,1)} %lift_in.1) | copy-start | bytes 98308
  5.5 0.8 %copy-start.4 = (bf16[256,64]{0,1:T(8,128)(2,1)S(1)}, bf16[256,64]{0,1:T(8,128)(2,1)}, u32[]{:S(2)}) copy-start(bf16[256,64]{0,1:T(8,128)(2,1)} %param.23) | copy-start | bytes 98308
  6.2 0.7 %copy-start.5 = (f32[256]{0:T(256)S(1)}, f32[256]{0:T(256)}, u32[]{:S(2)}) copy-start(f32[256]{0:T(256)} %param.15) | copy-start | bytes 3076
  6.9 0.7 %copy-start.6 = (s32[256]{0:T(256)S(1)}, s32[256]{0:T(256)}, u32[]{:S(2)}) copy-start(s32[256]{0:T(256)} %param.16) | copy-start | bytes 3076
  7.6 0.7 %copy-start.7 = (s32[256]{0:T(256)S(1)}, s32[256]{0:T(256)}, u32[]{:S(2)}) copy-start(s32[256]{0:T(256)} %param.17) | copy-start | bytes 3076
  8.3 0.7 %copy-start.8 = (s32[256]{0:T(256)S(1)}, s32[256]{0:T(256)}, u32[]{:S(2)}) copy-start(s32[256]{0:T(256)} %param.18) | copy-start | bytes 3076
  9.0 0.7 %copy-start.9 = (f32[256]{0:T(256)S(1)}, f32[256]{0:T(256)}, u32[]{:S(2)}) copy-start(f32[256]{0:T(256)} %param.19) | copy-start | bytes 3076
  9.6 0.7 %copy-start.10 = (f32[256]{0:T(256)S(1)}, f32[256]{0:T(256)}, u32[]{:S(2)}) copy-start(f32[256]{0:T(256)} %param.24) | copy-start | bytes 3076
  10.3 0.7 %copy-start.11 = (f32[256]{0:T(256)S(1)}, f32[256]{0:T(256)}, u32[]{:S(2)}) copy-start(f32[256]{0:T(256)} %param.25) | copy-start | bytes 3076

commit v3 on v2

--- a/solution.py
+++ b/solution.py
@@ -57,14 +57,37 @@
     return h + h * jnp.tanh(h)
 
 
-def kernel(
-    nb, nw, rows, nv, nc, lon,
-    x0, noise, sv, cell, owner, slot, weight, live, lift_in, conv_in, head, gain1, gain2,
-    out, innov,
-    x, lift, conv, g1, g2, sc, lifted, act, onehot, slothot, wmask, offmask,
-    tsend, psend, rowbuf, tilebuf, partbuf,
-    send_sem, recv_sem,
-):
+CHUNK = 64
+
+
+def layer(values, half_gain, emit):
+    nc, lon = values.shape
+    power = jnp.zeros((1, lon), F32)
+    for c in range(0, nc, CHUNK):
+        v = values[c:c + CHUNK, :]
+        power = power + jnp.sum(v * v, axis=0, keepdims=True)
+    scale = lax.rsqrt(power * (1.0 / nc) + 1e-06)
+    for c in range(0, nc, CHUNK):
+        g = half_gain[c:c + CHUNK, :]
+        h = values[c:c + CHUNK, :] * scale * jnp.concatenate([g] * (lon // 128), axis=1)
+        emit(c, h + h * jnp.tanh(h))
+
+
+def kernel(nb, nw, rows, nv, nc, lon, *refs):
+    inputs, (out, innov) = refs[:13], refs[13:15]
+    staged = refs[15:28]
+    (
+        x, lift, conv, g1, g2, sc, lifted, act, second, onehot, slothot, wmask, offmask,
+        tsend, psend, rowbuf, tilebuf, partbuf, send_sem, recv_sem, load_sem,
+    ) = refs[28:]
+    x0, noise, sv, cell, owner, slot, weight, _, lift_in, conv_in, head, gain1, gain2 = staged
+    live = inputs[7]
+    loads = [
+        pltpu.make_async_copy(source, target, load_sem.at[i])
+        for i, (source, target) in enumerate(zip(inputs, staged))
+    ]
+    for i in (3, 4, 5, 6, 2, 11, 12, 0, 8, 9, 10, 1):
+        loads[i].start()
     me = lax.axis_index("band")
     col = lax.axis_index("wt")
     left = lax.rem(col + nw - 1, nw)
@@ -100,6 +123,9 @@
                 greet(me + d, left)
                 greet(me + d, right)
 
+    for i in range(13):
+        if i not in (1, 7, 9, 10):
+            loads[i].wait()
     e = cell.shape[1]
     c = cell[...]
     alive = lax.broadcasted_iota(jnp.int32, (1, e), 1) < live[0]
@@ -126,11 +152,14 @@
             x[pl.ds(r * nv, nv), 128 * h:128 * (h + 1)] = x0[lines_of(r, h), :]
 
     lift[...] = lift_in[...].T
+    loads[9].wait()
     for t in range(9):
         conv[:, t * nc:(t + 1) * nc] = conv_in[t].T
     g1[...] = jnp.broadcast_to(0.5 * gain1[...], (128, nc)).T
     g2[...] = jnp.broadcast_to(0.5 * gain2[...], (128, nc)).T
 
+    loads[10].wait()
+    loads[1].wait()
     peers = 2
     for d in dists:
         peers = peers + jnp.where(exists(d), 3 if abs(d) == 1 else 1, 0)
@@ -193,60 +222,72 @@
         high, low = halves(values * offmask[...])
         part = nt(high, slothot[...]) + nt(low, slothot[...])
         psend[...] = jnp.where(row8 == 2 * REACH + 1, sv[...], part)
+
+        def widen(r, source, slot):
+            lifted[slot] = nn(lift[...], source)
+
+            def emit(c, f):
+                part = slice(c, c + CHUNK)
+                act[r, 1, part, :] = f.astype(BF16)
+                near, far = f[:, :128], f[:, lon - 128:]
+                a0, a1 = pltpu.roll(near, 1, 1), pltpu.roll(far, 1, 1)
+                b0, b1 = pltpu.roll(near, 127, 1), pltpu.roll(far, 127, 1)
+                act[r, 0, part, :128] = a0.astype(BF16)
+                act[r, 0, part, 128:] = jnp.where(lane == 0, a0, a1).astype(BF16)
+                act[r, 2, part, :128] = jnp.where(lane == 127, b1, b0).astype(BF16)
+                act[r, 2, part, 128:] = b1.astype(BF16)
+
+            layer(lifted.at[slot], g1, emit)
+
+        def patch(edge, which):
+            rim = silu_rms(nn(lift[...], edge.astype(BF16)), g1[...])
+            for r in which:
+                here = rim if r == 0 else pltpu.roll(rim, 128 - 2 * r, 1)
+                now = act[r, 0, :, :128].astype(F32)
+                act[r, 0, :, :128] = jnp.where(lane == 0, here, now).astype(BF16)
+                now = act[r, 2, :, 128:].astype(F32)
+                act[r, 2, :, 128:] = jnp.where(lane == 127, here, now).astype(BF16)
+
+        def convolve(r):
+            window = act[pl.ds(r, 3)].reshape(9 * nc, lon)
+            lifted[r] = lifted[r] + nn(conv[...], window)
+
+            def emit(c, f):
+                second[r, c:c + CHUNK, :] = f.astype(BF16)
+
+            layer(lifted.at[r], g2, emit)
+
+        widen(1, sc[0], 0)
         for d, copy in parts:
             when(d, copy.start)
-
-        def widen(r, f):
-            act[r, 1] = f.astype(BF16)
-            near, far = f[:, :128], f[:, lon - 128:]
-            a0, a1 = pltpu.roll(near, 1, 1), pltpu.roll(far, 1, 1)
-            b0, b1 = pltpu.roll(near, 127, 1), pltpu.roll(far, 127, 1)
-            act[r, 0, :, :128] = a0.astype(BF16)
-            act[r, 0, :, 128:] = jnp.where(lane == 0, a0, a1).astype(BF16)
-            act[r, 2, :, :128] = jnp.where(lane == 127, b1, b0).astype(BF16)
-            act[r, 2, :, 128:] = b1.astype(BF16)
-
-        half1 = g1[...]
-        wide1 = jnp.concatenate([half1, half1], axis=1)
-        for r in range(rows):
-            v = nn(lift[...], sc[r])
-            lifted[r] = v
-            widen(r + 1, silu_rms(v, wide1))
-
-        for d, copy in copies:
-            when(None if d is None else -d, copy.wait_recv)
+        for r in range(1, rows):
+            widen(r + 1, sc[r], r)
+
+        for d, copy in copies[:2]:
+            copy.wait_recv()
+        even = lane % 2 == 0
+        inner = jnp.logical_and(lane >= 1, lane <= 2 * rows)
+        edge = jnp.where(even, tilebuf[k, 0].astype(F32), tilebuf[k, 1].astype(F32))
+        patch(jnp.where(inner, edge, F32(0.0)), range(1, rows + 1))
+        for r in range(1, rows - 1):
+            convolve(r)
+
+        for d, copy in copies[2:]:
+            when(-d, copy.wait_recv)
         for r, i in ((0, 0), (rows + 1, 1)):
-            widen(r, silu_rms(nn(lift[...], rowbuf[k, i]), wide1))
-        t = [tilebuf[k, i].astype(F32) for i in range(6)]
-        edge = jnp.where(lane == 0, pltpu.roll(t[2], 128 - 2 * rows, 1), F32(0.0))
-        edge = jnp.where(lane == 127, pltpu.roll(t[3], 128 - 2 * rows, 1), edge)
-        inner = jnp.logical_and(lane >= 1, lane <= 2 * rows)
-        even = lane % 2 == 0
-        edge = jnp.where(jnp.logical_and(inner, even), t[0], edge)
-        edge = jnp.where(jnp.logical_and(inner, jnp.logical_not(even)), t[1], edge)
-        edge = jnp.where(lane == 2 * rows + 2, pltpu.roll(t[4], 2 * rows, 1), edge)
-        edge = jnp.where(lane == 2 * rows + 1, pltpu.roll(t[5], 2 * rows, 1), edge)
-        rim = silu_rms(nn(lift[...], edge.astype(BF16)), half1)
-        for r in range(rows + 2):
-            here = rim if r == 0 else pltpu.roll(rim, 128 - 2 * r, 1)
-            now = act[r, 0, :, :128].astype(F32)
-            act[r, 0, :, :128] = jnp.where(lane == 0, here, now).astype(BF16)
-            now = act[r, 2, :, 128:].astype(F32)
-            act[r, 2, :, 128:] = jnp.where(lane == 127, here, now).astype(BF16)
-
-        half2 = g2[...]
-        wide2 = jnp.concatenate([half2, half2], axis=1)
-        scores = []
-        for r in range(rows):
-            window = act[pl.ds(r, 3)].reshape(9 * nc, lon)
-            mixed = lifted[r] + nn(conv[...], window)
-            second = silu_rms(mixed, wide2).astype(BF16)
-            scores.append(nn(head[...], second))
+            widen(r, rowbuf[k, i], rows + i)
+        t = [tilebuf[k, i].astype(F32) for i in range(2, 6)]
+        edge = jnp.where(lane == 0, pltpu.roll(t[0], 128 - 2 * rows, 1), F32(0.0))
+        edge = jnp.where(lane == 127, pltpu.roll(t[1], 128 - 2 * rows, 1), edge)
+        edge = jnp.where(lane == 2 * rows + 2, pltpu.roll(t[2], 2 * rows, 1), edge)
+        edge = jnp.where(lane == 2 * rows + 1, pltpu.roll(t[3], 2 * rows, 1), edge)
+        patch(edge, (0, rows + 1))
+        convolve(0)
 
         for d, copy in parts:
             when(-d, copy.wait_recv)
-        mine = psend[...]
-        total = mine
+        convolve(rows - 1)
+        total = psend[...]
         observed = jnp.where(row8 == REACH, sv[...], F32(0.0))
         for d in dists:
             got = partbuf[k, d + SPAN]
@@ -260,7 +301,8 @@
         back = nn(high, slothot[...]) + nn(low, slothot[...])
         back = jnp.sum(back * offmask[...], axis=0, keepdims=True)
         high, low = halves(wmask[...] * back)
-        adjoint = nt(high, hot) + nt(low, hot)
+        adjoint = nt(high, onehot[...]) + nt(low, onehot[...])
+        scores = [nn(head[...], second[r]) for r in range(rows)]
 
         for r in range(rows):
             here = pl.ds(r * nv, nv)
@@ -300,23 +342,33 @@
     row = lambda a: a.reshape(1, -1)
     vmem = pl.BlockSpec(memory_space=pltpu.VMEM)
     count = 8 + 2 * SPAN
+    operands = (
+        x0, noise, row(station_values), row(entry_cell), row(entry_owner), row(entry_slot),
+        row(entry_weight), live_counts, lift_weight, conv_weight, head_weight.T,
+        row(first_gain), row(second_gain),
+    )
+    space = lambda i: pltpu.SMEM if i == 7 else pltpu.VMEM
     state, innov = pl.pallas_call(
         functools.partial(kernel, nb, nw, rows, nv, nc, lon),
         out_shape=(
             jax.ShapeDtypeStruct((lines, 128), F32),
             jax.ShapeDtypeStruct((1, stations), F32),
         ),
-        in_specs=[vmem] * 7 + [pl.BlockSpec(memory_space=pltpu.SMEM)] + [vmem] * 5,
+        in_specs=[
+            pl.BlockSpec(memory_space=pltpu.SMEM if i == 7 else pl.ANY)
+            for i in range(len(operands))
+        ],
         out_specs=(vmem, vmem),
-        scratch_shapes=[
+        scratch_shapes=[space(i)(a.shape, a.dtype) for i, a in enumerate(operands)] + [
             pltpu.VMEM((rows * nv, lon), F32),
             pltpu.VMEM((nc, nv), BF16),
             pltpu.VMEM((nc, 9 * nc), BF16),
             pltpu.VMEM((nc, 128), F32),
             pltpu.VMEM((nc, 128), F32),
             pltpu.VMEM((rows, nv, lon), BF16),
-            pltpu.VMEM((rows, nc, lon), F32),
+            pltpu.VMEM((rows + 2, nc, lon), F32),
             pltpu.VMEM((rows + 2, 3, nc, lon), BF16),
+            pltpu.VMEM((rows, nc, lon), BF16),
             pltpu.VMEM((lon, e), BF16),
             pltpu.VMEM((stations, e), BF16),
             pltpu.VMEM((rows * nv, e), F32),
@@ -328,15 +380,12 @@
             pltpu.VMEM((steps, 2 * SPAN + 1, 8, stations), F32),
             pltpu.SemaphoreType.DMA((count,)),
             pltpu.SemaphoreType.DMA((steps, count)),
+            pltpu.SemaphoreType.DMA((len(operands),)),
         ],
         compiler_params=pltpu.CompilerParams(
             collective_id=0, has_side_effects=True, vmem_limit_bytes=40 * 1024 * 1024
         ),
-    )(
-        x0, noise, row(station_values), row(entry_cell), row(entry_owner), row(entry_slot),
-        row(entry_weight), live_counts, lift_weight, conv_weight, head_weight.T,
-        row(first_gain), row(second_gain),
-    )
+    )(*operands)
     state = state.reshape(nv, sides, rows, 128).transpose(0, 2, 1, 3).reshape(nv, rows, lon)
     return state, innov.reshape(-1)
 

time: 51.8 us -> 44 us (0.85)
  Pallas kernels: 39 us -> 31.2 us
    pallas_call x1, Pallas kernels: 39 us -> 31.2 us  [per_device(): pl.pallas_call(functools.partial(kernel, nb, nw, rows, nv, nc, lon), out_...]
where the time goes in v3:
time: 44 us; the launch traced here: 43.5 us
  Pallas kernels  31.2 us (71%)
  local copies, waits for them, and re-layouts  11 us (25%)
  between operations  1.31 us (3%)
    pallas_call x1, Pallas kernels, per_device(): pl.pallas_call(functools.partial(kernel, nb, nw, rows, nv, nc, lon), out_...  31.2 us
    unnamed x26, local copies, waits for them, and re-layouts  11 us

profile of v3, /device:TPU:0, one launch (start us, length us, event | category | flops | bytes accessed | tf_op | source)
XLA Modules:
  0.0 43.5 jit_solution(5097295417995357056)
XLA Ops:
  1.3 0.0 copy-start
  1.3 1.3 %copy-done = bf16[9,256,256]{2,1,0:T(8,128)(2,1)S(1)} copy-done((bf16[9,256,256]{2,1,0:T(8,128)(2,1)S(1)}, bf16[9,256,256]{2,1,0:T(8,128)(2,1)}, u32[]{:S(2)}) %copy-start) | copy-done | bytes 1179672
  2.6 0.0 copy-start.1
  2.6 1.2 %copy-done.1 = f32[4,64,4,256]{3,2,1,0:T(4,128)S(1)} copy-done((f32[4,64,4,256]{3,2,1,0:T(4,128)S(1)}, f32[4,64,4,256]{3,2,1,0:T(4,128)}, u32[]{:S(2)}) %copy-start.1) | copy-done | bytes 1048600
  3.8 0.0 copy-start.2
  3.8 0.9 %copy-done.2 = f32[64,4,256]{2,1,0:T(4,128)S(1)} copy-done((f32[64,4,256]{2,1,0:T(4,128)S(1)}, f32[64,4,256]{2,1,0:T(4,128)}, u32[]{:S(2)}) %copy-start.2) | copy-done | bytes 262168
  4.7 0.0 copy-start.3
  4.7 0.8 %copy-done.3 = bf16[64,256]{1,0:T(8,128)(2,1)S(1)} copy-done((bf16[64,256]{1,0:T(8,128)(2,1)S(1)}, bf16[64,256]{1,0:T(8,128)(2,1)}, u32[]{:S(2)}) %copy-start.3) | copy-done | bytes 32792
  5.5 0.0 copy-start.4
  5.5 0.8 %copy-done.4 = bf16[256,64]{0,1:T(8,128)(2,1)S(1)} copy-done((bf16[256,64]{0,1:T(8,128)(2,1)S(1)}, bf16[256,64]{0,1:T(8,128)(2,1)}, u32[]{:S(2)}) %copy-start.4) | copy-done | bytes 32792
  6.2 0.0 copy-start.5
  6.2 0.7 %copy-done.5 = f32[256]{0:T(256)S(1)} copy-done((f32[256]{0:T(256)S(1)}, f32[256]{0:T(256)}, u32[]{:S(2)}) %copy-start.5) | copy-done | bytes 1048
  6.9 0.0 copy-start.6
  6.9 0.7 %copy-done.6 = s32[256]{0:T(256)S(1)} copy-done((s32[256]{0:T(256)S(1)}, s32[256]{0:T(256)}, u32[]{:S(2)}) %copy-start.6) | copy-done | bytes 1048
  7.6 0.0 copy-start.7
  7.6 0.7 %copy-done.7 = s32[256]{0:T(256)S(1)} copy-done((s32[256]{0:T(256)S(1)}, s32[256]{0:T(256)}, u32[]{:S(2)}) %copy-start.7) | copy-done | bytes 1048
  8.3 0.0 copy-start.8
  8.3 0.7 %copy-done.8 = s32[256]{0:T(256)S(1)} copy-done((s32[256]{0:T(256)S(1)}, s32[256]{0:T(256)}, u32[]{:S(2)}) %copy-start.8) | copy-done | bytes 1048
  9.0 0.0 copy-start.9
  9.0 0.7 %copy-done.9 = f32[256]{0:T(256)S(1)} copy-done((f32[256]{0:T(256)S(1)}, f32[256]{0:T(256)}, u32[]{:S(2)}) %copy-start.9) | copy-done | bytes 1048
  9.6 0.0 copy-start.10
  9.6 0.7 %copy-done.10 = f32[256]{0:T(256)S(1)} copy-done((f32[256]{0:T(256)S(1)}, f32[256]{0:T(256)}, u32[]{:S(2)}) %copy-start.10) | copy-done | bytes 1048
  10.3 0.0 copy-start.11
  10.3 0.7 %copy-done.11 = f32[256]{0:T(256)S(1)} copy-done((f32[256]{0:T(256)S(1)}, f32[256]{0:T(256)}, u32[]{:S(2)}) %copy-start.11) | copy-done | bytes 1048
  11.0 31.2 %shard_map.140 = (f32[512,128]{1,0:T(8,128)S(1)}, f32[1,256]{1,0:T(1,128)S(1)}) custom-call(f32[512,128]{1,0:T(8,128)S(1)} %bitcast.25, f32[4,512,128]{2,1,0:T(8,128)S(1)} %bitcast.24, f32[1,256]{1,0:T(1,128)S(1)} %bitcast.28, s32[1,256]{1,0:T(1,128)S(1)} %bitcast.29, s32[1,256]{1,0:T(1,128)S(1)} %bitcast.30, s32[1,256]{1,0:T(1,128)S(1)} %bitcast.31, ...), custom_call_target="tpu_custom_call" | custom-call | tf_op jit(solution)/shard_map/pallas_call | solution.py:351
  42.3 0.7 %copy.21 = f32[64,4,256]{2,1,0:T(4,128)} copy(f32[64,4,256]{2,1,0:T(4,128)S(1)} %bitcast.26) | data formatting | bytes 524288
  43.0 0.6 %copy.22 = f32[256]{0:T(256)} copy(f32[256]{0:T(256)S(1)} %bitcast.35) | data formatting | bytes 2048
Async XLA Ops:
  1.3 1.3 %copy-start = (bf16[9,256,256]{2,1,0:T(8,128)(2,1)S(1)}, bf16[9,256,256]{2,1,0:T(8,128)(2,1)}, u32[]{:S(2)}) copy-start(bf16[9,256,256]{2,1,0:T(8,128)(2,1)} %refs_9_.1) | copy-start | bytes 3538948
  2.6 1.2 %copy-start.1 = (f32[4,64,4,256]{3,2,1,0:T(4,128)S(1)}, f32[4,64,4,256]{3,2,1,0:T(4,128)}, u32[]{:S(2)}) copy-start(f32[4,64,4,256]{3,2,1,0:T(4,128)} %param.14) | copy-start | bytes 3145732
  3.8 0.9 %copy-start.2 = (f32[64,4,256]{2,1,0:T(4,128)S(1)}, f32[64,4,256]{2,1,0:T(4,128)}, u32[]{:S(2)}) copy-start(f32[64,4,256]{2,1,0:T(4,128)} %param.13) | copy-start | bytes 786436
  4.7 0.8 %copy-start.3 = (bf16[64,256]{1,0:T(8,128)(2,1)S(1)}, bf16[64,256]{1,0:T(8,128)(2,1)}, u32[]{:S(2)}) copy-start(bf16[64,256]{1,0:T(8,128)(2,1)} %refs_8_.1) | copy-start | bytes 98308
  5.5 0.8 %copy-start.4 = (bf16[256,64]{0,1:T(8,128)(2,1)S(1)}, bf16[256,64]{0,1:T(8,128)(2,1)}, u32[]{:S(2)}) copy-start(bf16[256,64]{0,1:T(8,128)(2,1)} %param.23) | copy-start | bytes 98308
  6.2 0.7 %copy-start.5 = (f32[256]{0:T(256)S(1)}, f32[256]{0:T(256)}, u32[]{:S(2)}) copy-start(f32[256]{0:T(256)} %param.15) | copy-start | bytes 3076
  6.9 0.7 %copy-start.6 = (s32[256]{0:T(256)S(1)}, s32[256]{0:T(256)}, u32[]{:S(2)}) copy-start(s32[256]{0:T(256)} %param.16) | copy-start | bytes 3076
  7.6 0.7 %copy-start.7 = (s32[256]{0:T(256)S(1)}, s32[256]{0:T(256)}, u32[]{:S(2)}) copy-start(s32[256]{0:T(256)} %param.17) | copy-start | bytes 3076
  8.3 0.7 %copy-start.8 = (s32[256]{0:T(256)S(1)}, s32[256]{0:T(256)}, u32[]{:S(2)}) copy-start(s32[256]{0:T(256)} %param.18) | copy-start | bytes 3076
  9.0 0.7 %copy-start.9 = (f32[256]{0:T(256)S(1)}, f32[256]{0:T(256)}, u32[]{:S(2)}) copy-start(f32[256]{0:T(256)} %param.19) | copy-start | bytes 3076
  9.6 0.7 %copy-start.10 = (f32[256]{0:T(256)S(1)}, f32[256]{0:T(256)}, u32[]{:S(2)}) copy-start(f32[256]{0:T(256)} %param.24) | copy-start | bytes 3076
  10.3 0.7 %copy-start.11 = (f32[256]{0:T(256)S(1)}, f32[256]{0:T(256)}, u32[]{:S(2)}) copy-start(f32[256]{0:T(256)} %param.25) | copy-start | bytes 3076

commit v4 on v3

--- a/solution.py
+++ b/solution.py
@@ -82,10 +82,10 @@
     ) = refs[28:]
     x0, noise, sv, cell, owner, slot, weight, _, lift_in, conv_in, head, gain1, gain2 = staged
     live = inputs[7]
-    loads = [
-        pltpu.make_async_copy(source, target, load_sem.at[i])
-        for i, (source, target) in enumerate(zip(inputs, staged))
-    ]
+    loads = {
+        i: pltpu.make_async_copy(inputs[i], staged[i], load_sem.at[i])
+        for i in range(len(inputs)) if i != 7
+    }
     for i in (3, 4, 5, 6, 2, 11, 12, 0, 8, 9, 10, 1):
         loads[i].start()
     me = lax.axis_index("band")
@@ -355,7 +355,7 @@
             jax.ShapeDtypeStruct((1, stations), F32),
         ),
         in_specs=[
-            pl.BlockSpec(memory_space=pltpu.SMEM if i == 7 else pl.ANY)
+            pl.BlockSpec(memory_space=pltpu.SMEM if i == 7 else pltpu.HBM)
             for i in range(len(operands))
         ],
         out_specs=(vmem, vmem),
@@ -383,7 +383,7 @@
             pltpu.SemaphoreType.DMA((len(operands),)),
         ],
         compiler_params=pltpu.CompilerParams(
-            collective_id=0, has_side_effects=True, vmem_limit_bytes=40 * 1024 * 1024
+            collective_id=0, has_side_effects=True, vmem_limit_bytes=58 * 1024 * 1024
         ),
     )(*operands)
     state = state.reshape(nv, sides, rows, 128).transpose(0, 2, 1, 3).reshape(nv, rows, lon)

time: 44 us -> 36 us (0.82)
  local copies, waits for them, and re-layouts: 11 us -> 2.9 us
    unnamed x26 -> x2, local copies, waits for them, and re-layouts: 11 us -> 2.9 us
where the time goes in v4:
time: 36 us; the launch traced here: 35.7 us
  Pallas kernels  31.5 us (88%)
  local copies, waits for them, and re-layouts  2.9 us (8%)
  between operations  1.29 us (4%)
    pallas_call x1, Pallas kernels, per_device(): pl.pallas_call(functools.partial(kernel, nb, nw, rows, nv, nc, lon), out_...  31.5 us
    unnamed x2, local copies, waits for them, and re-layouts  2.9 us

profile of v4, /device:TPU:0, one launch (start us, length us, event | category | flops | bytes accessed | tf_op | source)
XLA Modules:
  0.0 35.7 jit_solution(8480474122142287824)
XLA Ops:
  1.3 31.5 %shard_map.140 = (f32[512,128]{1,0:T(8,128)}, f32[1,256]{1,0:T(1,128)}) custom-call(f32[512,128]{1,0:T(8,128)} %bitcast.25, f32[4,512,128]{2,1,0:T(8,128)} %bitcast.24, f32[1,256]{1,0:T(1,128)} %bitcast.28, s32[1,256]{1,0:T(1,128)} %bitcast.29, s32[1,256]{1,0:T(1,128)} %bitcast.30, s32[1,256]{1,0:T(1,128)} %bitcast.31, f32[1,256]{1,0:T(1,128)} %bitcast.32, ...), custom_call_target="tpu_custom_call" | custom-call | tf_op jit(solution)/shard_map/pallas_call | solution.py:351
  32.8 1.7 %copy.21 = f32[64,4,256]{2,1,0:T(4,128)} copy(f32[64,4,256]{2,1,0:T(4,128)} %bitcast.26) | data formatting | bytes 524288
  34.5 1.2 %copy.22 = f32[256]{0:T(256)} copy(f32[256]{0:T(256)} %bitcast.35) | data formatting | bytes 2048
